TPU v7x, 32 devices: a whole 2x2x4 slice. The times are simulated.
32 devices in a mesh: dp: 4 (over z), ctx: 2 (over y), fsdp: 4 (over x, core).
Axes of the slice: x: 2, y: 2, z: 4, core: 2. Of those that a mesh axis runs over, the one named last changes fastest.
Arguments:
- tokens: bfloat16 [16, 1024, 2048], P(('dp', 'fsdp'), 'ctx'), may hold values from -6 to 6
- cotangent: bfloat16 [16, 1024, 2048], P(('dp', 'fsdp'), 'ctx'), may hold values from -6 to 6
- positions: int32 [16, 1024], P(('dp', 'fsdp'), 'ctx'), may hold values from 0 to 1023, as said below
- block_map: int32 [4], replicated, may hold values from 0 to 3, as said below
- w_query: bfloat16 [2048, 2048], P(('dp', 'fsdp')), may hold values from -0.125 to 0.125
- w_key: bfloat16 [2048, 1024], P(('dp', 'fsdp')), may hold values from -0.125 to 0.125
- w_value: bfloat16 [2048, 1024], P(('dp', 'fsdp')), may hold values from -0.125 to 0.125
- w_output: bfloat16 [2048, 2048], P(('dp', 'fsdp')), may hold values from -1 to 1
- w_gate: bfloat16 [2048, 6144], P(('dp', 'fsdp')), may hold values from -0.125 to 0.125
- w_up: bfloat16 [2048, 6144], P(('dp', 'fsdp')), may hold values from -0.125 to 0.125
- w_down: bfloat16 [6144, 2048], P(('dp', 'fsdp')), may hold values from -0.078125 to 0.078125
- gain_attn: bfloat16 [2048], P(('dp', 'fsdp')), may hold values from 0.5 to 1.5
- gain_mlp: bfloat16 [2048], P(('dp', 'fsdp')), may hold values from 0.5 to 1.5
- gain_query: bfloat16 [128], P(('dp', 'fsdp')), may hold values from 0.5 to 1.5
- gain_key: bfloat16 [128], P(('dp', 'fsdp')), may hold values from 0.5 to 1.5
Outputs:
- output: bfloat16 [16, 1024, 2048], P(('dp', 'fsdp'), 'ctx')
- grad_tokens: bfloat16 [16, 1024, 2048], P(('dp', 'fsdp'), 'ctx')
- grad_query: float32 [2048, 2048], P(('dp', 'fsdp'))
- grad_key: float32 [2048, 1024], P(('dp', 'fsdp'))
- grad_value: float32 [2048, 1024], P(('dp', 'fsdp'))
- grad_output: float32 [2048, 2048], P(('dp', 'fsdp'))
- grad_gate: float32 [2048, 6144], P(('dp', 'fsdp'))
- grad_up: float32 [2048, 6144], P(('dp', 'fsdp'))
- grad_down: float32 [6144, 2048], P(('dp', 'fsdp'))
- grad_gain_attn: float32 [2048], P(('dp', 'fsdp'))
- grad_gain_mlp: float32 [2048], P(('dp', 'fsdp'))
- grad_gain_query: float32 [128], P(('dp', 'fsdp'))
- grad_gain_key: float32 [128], P(('dp', 'fsdp'))
Inputs may be any that keep to these rules, and one draw needn't show every extreme that they name: `block_map`: entries 2c and 2c + 1 are the two blocks held by the c-th device of ctx, a pair b and 3 - b in either order; every block appears once. `positions`: in each sequence's natural token order a position counts up by one from 0, starting again at each document's first token; the first token starts a document; the first sequence is one document; rows are laid out in the order of block_map.
All inputs are finite; a program needn't handle non-finite values.
Results may differ from a plain program's by a relative error of at most 0.02.
Values may be sent and summed in bfloat16 or wider, within the bound.
A program may use at most 512 MiB of HBM per device.

v0:
```python
import jax
import jax.numpy as jnp
from jax import lax
from jax.sharding import PartitionSpec as P

HEADS = 16
KV_HEADS = 8
HEAD_DIM = 128


EPS = 1e-06
THETA = 1000000.0


def product(left, right):
    return jnp.dot(left, right, preferred_element_type=jnp.float32)


def back_product(left, right):
    return lax.dot_general(
        left, right, (((1,), (1,)), ((), ())), preferred_element_type=jnp.float32
    )


def rms_scale(values, gain):
    return values * lax.rsqrt(jnp.mean(values * values, axis=-1, keepdims=True) + EPS) * gain


def rope_tables(positions):
    half = HEAD_DIM // 2
    freqs = THETA ** (-(jnp.arange(half, dtype=jnp.float32) * 2.0 / HEAD_DIM))
    angles = positions.astype(jnp.float32)[..., None] * freqs
    return (jnp.cos(angles), jnp.sin(angles))


def rotate(values, cosine, sine):
    half = values.shape[-1] // 2
    first = values[..., :half]
    second = values[..., half:]
    cos_b = cosine[..., None, :]
    sin_b = sine[..., None, :]
    return jnp.concatenate(
        [first * cos_b - second * sin_b, second * cos_b + first * sin_b], axis=-1
    )


def head_post(linear, gain, cosine, sine, heads, factor):
    shaped = linear.reshape(linear.shape[:-1] + (heads, HEAD_DIM))
    return rotate(rms_scale(shaped, gain), cosine, sine) * factor


def shard_grad(left, right):
    return lax.psum_scatter(
        lax.dot_general(
            left, right, (((0,), (0,)), ((), ())), preferred_element_type=jnp.float32
        ).astype(jnp.bfloat16),
        ("dp", "fsdp"),
        scatter_dimension=0,
        tiled=True,
    ).astype(jnp.float32)


def on_device(
    tokens,
    cotangent,
    positions,
    block_map,
    w_query,
    w_key,
    w_value,
    w_output,
    w_gate,
    w_up,
    w_down,
    gain_attn,
    gain_mlp,
    gain_query,
    gain_key,
):
    seq_count, local_rows, width = tokens.shape
    block = local_rows // 2
    total_len = block * 2 * lax.axis_size("ctx")
    row_count = seq_count * local_rows
    group = HEADS // KV_HEADS
    ctx_rank = lax.axis_index("ctx")
    own_blocks = lax.dynamic_slice_in_dim(block_map, 2 * ctx_rank, 2)
    query_index = (
        jnp.repeat(own_blocks, block) * block + jnp.arange(local_rows, dtype=jnp.int32) % block
    )
    key_index = (
        jnp.repeat(block_map, block) * block + jnp.arange(total_len, dtype=jnp.int32) % block
    )
    allowed = key_index[None, :] <= query_index[:, None]
    cosine, sine = rope_tables(positions)
    wq_all, wk_all, wv_all, wo_all, ga_all, gq_all, gk_all = (
        lax.all_gather(w_query, ("dp", "fsdp"), axis=0, tiled=True),
        lax.all_gather(w_key, ("dp", "fsdp"), axis=0, tiled=True),
        lax.all_gather(w_value, ("dp", "fsdp"), axis=0, tiled=True),
        lax.all_gather(w_output, ("dp", "fsdp"), axis=0, tiled=True),
        lax.all_gather(gain_attn, ("dp", "fsdp"), axis=0, tiled=True),
        lax.all_gather(gain_query, ("dp", "fsdp"), axis=0, tiled=True),
        lax.all_gather(gain_key, ("dp", "fsdp"), axis=0, tiled=True),
    )

    def post_pair(q_in, k_in, gq_in, gk_in):
        q_rot = head_post(
            q_in.reshape(seq_count, local_rows, HEADS * HEAD_DIM),
            gq_in,
            cosine,
            sine,
            HEADS,
            HEAD_DIM ** (-0.5),
        )
        k_rot = head_post(
            k_in.reshape(seq_count, local_rows, KV_HEADS * HEAD_DIM),
            gk_in,
            cosine,
            sine,
            KV_HEADS,
            1.0,
        )
        return (q_rot, k_rot)

    x_flat = tokens.reshape(row_count, width).astype(jnp.float32)
    h1_full, norm1_pull = jax.vjp(rms_scale, x_flat, ga_all.astype(jnp.float32))
    h1 = h1_full.astype(jnp.bfloat16)
    q_lin = product(h1, wq_all)
    k_lin = product(h1, wk_all)
    values = product(h1, wv_all).astype(jnp.bfloat16)
    (q_rot, k_rot), post_pull = jax.vjp(
        post_pair, q_lin, k_lin, gq_all.astype(jnp.float32), gk_all.astype(jnp.float32)
    )
    q_groups = q_rot.astype(jnp.bfloat16).reshape(seq_count, local_rows, KV_HEADS, group, HEAD_DIM)
    k_local = k_rot.reshape(seq_count, local_rows, KV_HEADS * HEAD_DIM).astype(jnp.bfloat16)
    v_local = values.reshape(seq_count, local_rows, KV_HEADS * HEAD_DIM)
    keys_all, values_all = (
        lax.all_gather(k_local, "ctx", axis=1, tiled=True),
        lax.all_gather(v_local, "ctx", axis=1, tiled=True),
    )

    def attend(head_index):
        query_head = lax.dynamic_index_in_dim(q_groups, head_index, 2, keepdims=False)
        key_head = lax.dynamic_slice_in_dim(keys_all, head_index * HEAD_DIM, HEAD_DIM, 2)
        value_head = lax.dynamic_slice_in_dim(values_all, head_index * HEAD_DIM, HEAD_DIM, 2)
        scores = jnp.einsum(
            "sqgd,skd->sgqk", query_head, key_head, preferred_element_type=jnp.float32
        )
        scores = jnp.where(allowed, scores, -1e30)
        highest = jnp.max(scores, axis=-1, keepdims=True)
        exponent = jnp.exp(scores - highest)
        total = jnp.sum(exponent, axis=-1, keepdims=True)
        probs = (exponent / total).astype(jnp.bfloat16)
        attended_head = jnp.einsum(
            "sgqk,skd->sqgd", probs, value_head, preferred_element_type=jnp.float32
        )
        return (attended_head, (highest + jnp.log(total))[..., 0])

    outs_heads, log_totals = lax.map(attend, jnp.arange(KV_HEADS))
    attended = (
        jnp.moveaxis(outs_heads, 0, 2).reshape(row_count, HEADS * HEAD_DIM).astype(jnp.bfloat16)
    )
    x_mid = x_flat + product(attended, wo_all)
    wg_all, wu_all, wd_all, gm_all = (
        lax.all_gather(w_gate, ("dp", "fsdp"), axis=0, tiled=True),
        lax.all_gather(w_up, ("dp", "fsdp"), axis=0, tiled=True),
        lax.all_gather(w_down, ("dp", "fsdp"), axis=0, tiled=True),
        lax.all_gather(gain_mlp, ("dp", "fsdp"), axis=0, tiled=True),
    )
    h2_full, norm2_pull = jax.vjp(rms_scale, x_mid, gm_all.astype(jnp.float32))
    h2 = h2_full.astype(jnp.bfloat16)
    gate = product(h2, wg_all)
    upper = product(h2, wu_all)
    sigmoid_gate = 1.0 / (1.0 + jnp.exp(-gate))
    hidden = (gate * sigmoid_gate * upper).astype(jnp.bfloat16)
    output = (x_mid + product(hidden, wd_all)).astype(jnp.bfloat16).reshape(tokens.shape)
    wg_all, wu_all, wd_all, gm_all = (
        lax.all_gather(w_gate, ("dp", "fsdp"), axis=0, tiled=True),
        lax.all_gather(w_up, ("dp", "fsdp"), axis=0, tiled=True),
        lax.all_gather(w_down, ("dp", "fsdp"), axis=0, tiled=True),
        lax.all_gather(gain_mlp, ("dp", "fsdp"), axis=0, tiled=True),
    )
    d_out = cotangent.reshape(row_count, width)
    d_hidden = back_product(d_out, wd_all)
    d_gate = (d_hidden * upper * sigmoid_gate * (1.0 + gate * (1.0 - sigmoid_gate))).astype(
        jnp.bfloat16
    )
    d_upper = (d_hidden * gate * sigmoid_gate).astype(jnp.bfloat16)
    d_h2 = back_product(d_gate, wg_all) + back_product(d_upper, wu_all)
    d_mid_part, d_gain_mlp = norm2_pull(d_h2)
    d_mid = d_out.astype(jnp.float32) + d_mid_part
    d_branch = d_mid.astype(jnp.bfloat16)
    grad_down = shard_grad(hidden, d_out)
    grad_gate = shard_grad(h2, d_gate)
    grad_up = shard_grad(h2, d_upper)
    wq_all, wk_all, wv_all, wo_all, ga_all, gq_all, gk_all = (
        lax.all_gather(w_query, ("dp", "fsdp"), axis=0, tiled=True),
        lax.all_gather(w_key, ("dp", "fsdp"), axis=0, tiled=True),
        lax.all_gather(w_value, ("dp", "fsdp"), axis=0, tiled=True),
        lax.all_gather(w_output, ("dp", "fsdp"), axis=0, tiled=True),
        lax.all_gather(gain_attn, ("dp", "fsdp"), axis=0, tiled=True),
        lax.all_gather(gain_query, ("dp", "fsdp"), axis=0, tiled=True),
        lax.all_gather(gain_key, ("dp", "fsdp"), axis=0, tiled=True),
    )
    d_attended = back_product(d_branch, wo_all).astype(jnp.bfloat16)
    grad_output = shard_grad(attended, d_branch)
    d_groups = d_attended.reshape(seq_count, local_rows, KV_HEADS, group, HEAD_DIM)

    def attend_back(items):
        head_index, log_head = items
        query_head = lax.dynamic_index_in_dim(q_groups, head_index, 2, keepdims=False)
        grad_head = lax.dynamic_index_in_dim(d_groups, head_index, 2, keepdims=False)
        key_head = lax.dynamic_slice_in_dim(keys_all, head_index * HEAD_DIM, HEAD_DIM, 2)
        value_head = lax.dynamic_slice_in_dim(values_all, head_index * HEAD_DIM, HEAD_DIM, 2)
        scores = jnp.einsum(
            "sqgd,skd->sgqk", query_head, key_head, preferred_element_type=jnp.float32
        )
        probs = jnp.where(allowed, jnp.exp(scores - log_head[..., None]), 0.0)
        d_probs = jnp.einsum(
            "sqgd,skd->sgqk", grad_head, value_head, preferred_element_type=jnp.float32
        )
        inner = jnp.sum(d_probs * probs, axis=-1, keepdims=True)
        d_scores = (probs * (d_probs - inner)).astype(jnp.bfloat16)
        d_query = jnp.einsum(
            "sgqk,skd->sqgd", d_scores, key_head, preferred_element_type=jnp.float32
        )
        d_key = jnp.einsum(
            "sgqk,sqgd->skd", d_scores, query_head, preferred_element_type=jnp.float32
        )
        d_value = jnp.einsum(
            "sgqk,sqgd->skd",
            probs.astype(jnp.bfloat16),
            grad_head,
            preferred_element_type=jnp.float32,
        )
        return (d_query, d_key, d_value)

    dq_heads, dk_heads, dv_heads = lax.map(attend_back, (jnp.arange(KV_HEADS), log_totals))
    dq_rot = jnp.moveaxis(dq_heads, 0, 2).reshape(seq_count, local_rows, HEADS, HEAD_DIM)
    dk_whole = jnp.moveaxis(dk_heads, 0, 2).reshape(seq_count, total_len, KV_HEADS * HEAD_DIM)
    dv_whole = jnp.moveaxis(dv_heads, 0, 2).reshape(seq_count, total_len, KV_HEADS * HEAD_DIM)
    d_keys, d_values = (
        lax.psum_scatter(
            dk_whole.astype(jnp.bfloat16), "ctx", scatter_dimension=1, tiled=True
        ).astype(jnp.float32),
        lax.psum_scatter(
            dv_whole.astype(jnp.bfloat16), "ctx", scatter_dimension=1, tiled=True
        ).astype(jnp.float32),
    )
    d_values_low = d_values.reshape(row_count, KV_HEADS * HEAD_DIM).astype(jnp.bfloat16)
    dq_lin, dk_lin, d_gain_query, d_gain_key = post_pull(
        (dq_rot, d_keys.reshape(seq_count, local_rows, KV_HEADS, HEAD_DIM))
    )
    dq_low = dq_lin.astype(jnp.bfloat16)
    dk_low = dk_lin.astype(jnp.bfloat16)
    d_h1 = (
        back_product(dq_low, wq_all)
        + back_product(dk_low, wk_all)
        + back_product(d_values_low, wv_all)
    )
    d_input_part, d_gain_attn = norm1_pull(d_h1)
    grad_tokens = (d_mid + d_input_part).astype(jnp.bfloat16).reshape(tokens.shape)
    grad_query = shard_grad(h1, dq_low)
    grad_key = shard_grad(h1, dk_low)
    grad_value = shard_grad(h1, d_values_low)
    gain_attn_part, gain_mlp_part, gain_query_part, gain_key_part = (
        lax.psum_scatter(d_gain_attn, ("dp", "fsdp"), scatter_dimension=0, tiled=True),
        lax.psum_scatter(d_gain_mlp, ("dp", "fsdp"), scatter_dimension=0, tiled=True),
        lax.psum_scatter(d_gain_query, ("dp", "fsdp"), scatter_dimension=0, tiled=True),
        lax.psum_scatter(d_gain_key, ("dp", "fsdp"), scatter_dimension=0, tiled=True),
    )
    summed = (
        lax.psum(grad_query.astype(jnp.bfloat16), "ctx").astype(jnp.float32),
        lax.psum(grad_key.astype(jnp.bfloat16), "ctx").astype(jnp.float32),
        lax.psum(grad_value.astype(jnp.bfloat16), "ctx").astype(jnp.float32),
        lax.psum(grad_output.astype(jnp.bfloat16), "ctx").astype(jnp.float32),
        lax.psum(grad_gate.astype(jnp.bfloat16), "ctx").astype(jnp.float32),
        lax.psum(grad_up.astype(jnp.bfloat16), "ctx").astype(jnp.float32),
        lax.psum(grad_down.astype(jnp.bfloat16), "ctx").astype(jnp.float32),
        lax.psum(gain_attn_part.astype(jnp.bfloat16), "ctx").astype(jnp.float32),
        lax.psum(gain_mlp_part.astype(jnp.bfloat16), "ctx").astype(jnp.float32),
        lax.psum(gain_query_part.astype(jnp.bfloat16), "ctx").astype(jnp.float32),
        lax.psum(gain_key_part.astype(jnp.bfloat16), "ctx").astype(jnp.float32),
    )
    return (
        output,
        grad_tokens,
        summed[0],
        summed[1],
        summed[2],
        summed[3],
        summed[4],
        summed[5],
        summed[6],
        summed[7],
        summed[8],
        summed[9],
        summed[10],
    )


def solution(mesh):
    return jax.shard_map(
        on_device,
        mesh=mesh,
        in_specs=(
            P(("dp", "fsdp"), "ctx", None),
            P(("dp", "fsdp"), "ctx", None),
            P(("dp", "fsdp"), "ctx"),
            P(),
            P(("dp", "fsdp"), None),
            P(("dp", "fsdp"), None),
            P(("dp", "fsdp"), None),
            P(("dp", "fsdp"), None),
            P(("dp", "fsdp"), None),
            P(("dp", "fsdp"), None),
            P(("dp", "fsdp"), None),
            P(("dp", "fsdp")),
            P(("dp", "fsdp")),
            P(("dp", "fsdp")),
            P(("dp", "fsdp")),
        ),
        out_specs=(
            P(("dp", "fsdp"), "ctx", None),
            P(("dp", "fsdp"), "ctx", None),
            P(("dp", "fsdp"), None),
            P(("dp", "fsdp"), None),
            P(("dp", "fsdp"), None),
            P(("dp", "fsdp"), None),
            P(("dp", "fsdp"), None),
            P(("dp", "fsdp"), None),
            P(("dp", "fsdp"), None),
            P(("dp", "fsdp")),
            P(("dp", "fsdp")),
            P(("dp", "fsdp")),
            P(("dp", "fsdp")),
        ),
        check_vma=False,
    )
```

profile of v0, /device:TPU:0, one launch (start us, length us, event | category | flops | bytes accessed | tf_op | source)
XLA Modules:
  0.0 2296.2 jit_solution(4219205483710552875)
XLA Ops:
  9.5 23.1 %all-gather.1 = bf16[16,1,128]{2,1,0:T(2,128)(2,1)S(1)} all-gather(bf16[1,1,128]{2,1,0:T(2,128)(2,1)} %bitcast.450), channel_id=1, replica_groups=mesh['dp'=4,'ctx'=2,'fsdp'=4] {'dp','fsdp'}, dimensions={0}, use_global_device_ids=true | all-gather | bytes 4352 | tf_op jit(solution)/shard_map/all_gather | solution.py:100
  37.0 30.5 %all-reduce.11 = (bf16[128]{0:T(256)(128)(2,1)S(1)}, bf16[128]{0:T(256)(128)(2,1)S(1)}) all-reduce(bf16[128]{0:T(256)(128)(2,1)S(1)} %dynamic-update-slice, bf16[128]{0:T(256)(128)(2,1)S(1)} %dynamic-update-slice.1), channel_id=1, replica_groups=mesh['dp'=4,'ctx'=2,'fsdp'=4] {'dp','fsdp'}, use_global_device_ids=true, to_apply=%add.4 | all-reduce | flops 256 | bytes 1024
  83.7 31.4 %all-gather.13.cloned.1.call-done = bf16[2048,1024]{1,0:T(8,128)(2,1)} async-done(((bf16[128,1024]{1,0:T(8,128)(2,1)}), bf16[2048,1024]{1,0:T(8,128)(2,1)}) %all-gather.13.cloned.1.call-update) | async-done | bytes 4194320 | tf_op jit(solution)/shard_map/all_gather | solution.py:98
  123.9 19.3 all-gather.2
  144.7 46.1 %all-gather.19.cloned.1.call-done = bf16[2048,2048]{1,0:T(8,128)(2,1)} async-done(((bf16[128,2048]{1,0:T(8,128)(2,1)}), bf16[2048,2048]{1,0:T(8,128)(2,1)}) %all-gather.19.cloned.1.call-update) | async-done | bytes 8388624 | tf_op jit(solution)/shard_map/all_gather | solution.py:96
  211.6 12.5 all-gather.17.cloned.1.call-done
  224.2 35.1 %all-gather.29.cloned.1.call-done = bf16[1024,1024]{1,0:T(8,128)(2,1)} async-done(((bf16[512,1024]{1,0:T(8,128)(2,1)}), bf16[1024,1024]{1,0:T(8,128)(2,1)}) %all-gather.29.cloned.1.call-update) | async-done | bytes 2097168 | tf_op jit(solution)/shard_map/all_gather | solution.py:138
  259.3 79.1 %while.30 = (s32[]{:T(128)}, bf16[8,1,512,2,128]{2,4,3,1,0:T(8,128)(2,1)}, f32[8,1,2,512]{3,2,1,0:T(2,128)}, s32[8]{0:T(128)S(1)}, bf16[1,1024,1024]{2,1,0:T(8,1...) while((s32[]{:T(128)}, ...), condition=%wide.region_6.7_spmd.clone.clone, body=%wide.region_3.6_spmd.clone.sunk.clone | while | flops 546831360 | bytes 16030917 | solution.py:158
  352.6 112.2 %all-gather.23.cloned.1.call-done = bf16[2048,6144]{1,0:T(8,128)(2,1)} async-done(((bf16[128,6144]{1,0:T(8,128)(2,1)}), bf16[2048,6144]{1,0:T(8,128)(2,1)}) %all-gather.23.cloned.1.call-update) | async-done | bytes 25165840 | tf_op jit(solution)/shard_map/all_gather | solution.py:164
  464.7 20.7 fusion.128
  485.5 109.5 %all-gather.25.cloned.1.call-done = bf16[2048,6144]{1,0:T(8,128)(2,1)} async-done(((bf16[128,6144]{1,0:T(8,128)(2,1)}), bf16[2048,6144]{1,0:T(8,128)(2,1)}) %all-gather.25.cloned.1.call-update) | async-done | bytes 25165840 | tf_op jit(solution)/shard_map/all_gather | solution.py:165
  595.0 20.6 fusion.129
  615.5 109.6 %all-gather.27.cloned.1.call-done = bf16[6144,2048]{1,0:T(8,128)(2,1)} async-done(((bf16[384,2048]{1,0:T(8,128)(2,1)}), bf16[6144,2048]{1,0:T(8,128)(2,1)}) %all-gather.27.cloned.1.call-update) | async-done | bytes 25165840 | tf_op jit(solution)/shard_map/all_gather | solution.py:166
  725.2 30.4 %multiply_convert_fusion = (bf16[512,6144]{1,0:T(8,128)(2,1)}, bf16[512,6144]{1,0:T(8,128)(2,1)}, bf16[512,6144]{1,0:T(8,128)(2,1)}) fusion(f32[512,6144]{1,0:T(8,128)} %fusion.128, f32[512,6144]{1,0:T(8,128)} %fusion.129, bf16[6144,2048]{1,0:T(8,128)(2,1)} %all-gather.27.cloned.1.call-done, bf16[1,512,2048]{2,1,0:T(8,128)(2,1)} %param.20), kind=kOutput, calls=%fused_computation.68 | convolution fusion | flops 12935233536 | bytes 71303168 | tf_op jit(solution)/shard_map/dot_general | solution.py:20
  755.5 21.1 fusion.130
  776.7 21.3 multiply_reduce_fusion.1
  813.6 130.3 %while.31 = (s32[]{:T(128)}, f32[8,1,512,2,128]{2,4,3,1,0:T(8,128)}, bf16[8,1,1024,128]{2,3,0,1:T(8,128)(2,1)}, bf16[8,1,1024,128]{2,3,0,1:T(8,128)(2,1)}, s32[8...) while((s32[]{:T(128)}, ...), condition=%wide.region_11.12_spmd.clone.clone, body=%wide.region_9.11_spmd.clone.sunk.clone | while | flops 1355283456 | bytes 37523180 | solution.py:237
  944.7 31.2 %reduce-scatter.10.cloned.1.call-done = bf16[1,512,1024]{1,2,0:T(8,128)(2,1)} async-done(((bf16[1,1024,1024]{1,2,0:T(8,128)(2,1)}), bf16[1,512,1024]{1,2,0:T(8,128)(2,1)}) %reduce-scatter.10.cloned.1.call-update) | async-done | bytes 1048592 | tf_op jit(solution)/shard_map/reduce_scatter | solution.py:242
  998.6 12.1 reduce-scatter.12.cloned.1.call-done
  1070.4 19.6 convolution_convert_fusion.2
  1090.0 19.4 convolution_convert_fusion.1
  1111.1 19.4 convolution_convert_fusion
  1132.1 30.6 %reduce-scatter.18.cloned.1.call-done = bf16[128,1024]{1,0:T(8,128)(2,1)} async-done(((bf16[2048,1024]{1,0:T(8,128)(2,1)}), bf16[128,1024]{1,0:T(8,128)(2,1)}) %reduce-scatter.18.cloned.1.call-update) | async-done | bytes 262160 | tf_op jit(solution)/shard_map/reduce_scatter | solution.py:53
  1162.7 107.6 %reduce-scatter.14.cloned.1.call-done = bf16[128,2048]{1,0:T(8,128)(2,1)} async-done(((bf16[2048,2048]{1,0:T(8,128)(2,1)}), bf16[128,2048]{1,0:T(8,128)(2,1)}) %reduce-scatter.14.cloned.1.call-update) | async-done | bytes 524304 | tf_op jit(solution)/shard_map/reduce_scatter | solution.py:53
  1270.3 108.3 %reduce-scatter.20.cloned.1.call-done = bf16[128,2048]{1,0:T(8,128)(2,1)} async-done(((bf16[2048,2048]{1,0:T(8,128)(2,1)}), bf16[128,2048]{1,0:T(8,128)(2,1)}) %reduce-scatter.20.cloned.1.call-update) | async-done | bytes 524304 | tf_op jit(solution)/shard_map/reduce_scatter | solution.py:53
  1378.6 247.7 %reduce-scatter.22.cloned.1.call-done = bf16[128,6144]{1,0:T(8,128)(2,1)} async-done(((bf16[2048,6144]{1,0:T(8,128)(2,1)}), bf16[128,6144]{1,0:T(8,128)(2,1)}) %reduce-scatter.22.cloned.1.call-update) | async-done | bytes 1572880 | tf_op jit(solution)/shard_map/reduce_scatter | solution.py:53
  1626.3 247.0 %reduce-scatter.24.cloned.1.call-done = bf16[128,6144]{1,0:T(8,128)(2,1)} async-done(((bf16[2048,6144]{1,0:T(8,128)(2,1)}), bf16[128,6144]{1,0:T(8,128)(2,1)}) %reduce-scatter.24.cloned.1.call-update) | async-done | bytes 1572880 | tf_op jit(solution)/shard_map/reduce_scatter | solution.py:53
  1873.3 246.9 %reduce-scatter.26.cloned.1.call-done = bf16[384,2048]{1,0:T(8,128)(2,1)} async-done(((bf16[6144,2048]{1,0:T(8,128)(2,1)}), bf16[384,2048]{1,0:T(8,128)(2,1)}) %reduce-scatter.26.cloned.1.call-update) | async-done | bytes 1572880 | tf_op jit(solution)/shard_map/reduce_scatter | solution.py:53
  2120.3 21.4 fusion.83
  2150.6 12.1 fusion.70
  2162.7 59.9 %all-reduce.10 = (bf16[2048]{0:T(1024)(128)(2,1)S(1)}, bf16[2048]{0:T(1024)(128)(2,1)S(1)}, bf16[128]{0:T(256)(128)(2,1)S(1)}, bf16[128]{0:T(256)(128)(2,1)S(1)}) all-reduce(f32[2048]{0:T(1024)S(1)} %get-tuple-element.281, f32[2048]{0:T(1024)S(1)} %copy-done.56, ...), channel_id=12, replica_groups=mesh['dp'=4,'ctx'=2,'fsdp'=4] {'dp','fsdp'}, use_global_device_ids=true, to_apply=%region_32.33.clone | all-reduce | flops 4352 | bytes 26112
  2235.9 41.9 %all-reduce.16.cloned.1.call-done = (bf16[128,2048]{1,0:T(8,128)(2,1)}, bf16[128,1024]{1,0:T(8,128)(2,1)}, bf16[128,1024]{1,0:T(8,128)(2,1)}, bf16[128,2048]{1,0...) async-done(((bf16[128,2048]{1,0:T(8,128)(2,1)}, bf16[128,1024]{1,0:T(8,128)(2,1)}, bf16[128,1024]{1,0:T(8,128)(2,1)}, ...) | async-done | bytes 6291472 | tf_op jit(solution)/shard_map/psum | solution.py:272
  (406 shorter events, 367.8 us)
Async XLA Ops:
  7.2 64.1 %all-gather.15.cloned.1.call-start = ((), (), s32[]{:S(2)}) async-start(), calls=%async_computation.10 | async-start | bytes 4456448 | tf_op jit(solution)/shard_map/all_gather | solution.py:97
  7.9 107.2 %all-gather.13.cloned.1.call-start = ((), (), s32[]{:S(2)}) async-start(), calls=%async_computation.9 | async-start | bytes 4456448 | tf_op jit(solution)/shard_map/all_gather | solution.py:98
  8.7 182.1 %all-gather.19.cloned.1.call-start = ((), (), s32[]{:S(2)}) async-start(), calls=%async_computation.12 | async-start | bytes 8912896 | tf_op jit(solution)/shard_map/all_gather | solution.py:96
  9.4 214.8 %all-gather.17.cloned.1.call-start = ((), (), s32[]{:S(2)}) async-start(), calls=%async_computation.11 | async-start | bytes 3145728 | tf_op jit(solution)/shard_map/all_gather | solution.py:137
  32.6 158.2 %copy-start.46 = (f32[16,1,128]{2,1,0:T(1,128)}, f32[16,1,128]{2,1,0:T(1,128)S(1)}, u32[]{:S(2)}) copy-start(f32[16,1,128]{2,1,0:T(1,128)S(1)} %convert_element_type.303) | copy-start | bytes 24580
  70.2 120.6 %copy-start.51 = (f32[512]{0:T(512)}, f32[512]{0:T(512)S(1)}, u32[]{:S(2)}) copy-start(f32[512]{0:T(512)S(1)} %fusion.117) | copy-start | bytes 6148
  71.2 135.0 %copy-start.16 = (f32[512,64]{1,0:T(8,128)}, f32[512,64]{1,0:T(8,128)S(1)}, u32[]{:S(2)}) copy-start(f32[512,64]{1,0:T(8,128)S(1)} %get-tuple-element.361) | copy-start | bytes 393220
  71.2 135.0 %copy-start.18 = (f32[512,64]{1,0:T(8,128)}, f32[512,64]{1,0:T(8,128)S(1)}, u32[]{:S(2)}) copy-start(f32[512,64]{1,0:T(8,128)S(1)} %get-tuple-element.362) | copy-start | bytes 393220
  79.8 35.4 %copy-start.12 = (bf16[1,512,2048]{2,1,0:T(8,128)(2,1)S(1)}, bf16[1,512,2048]{2,1,0:T(8,128)(2,1)}, u32[]{:S(2)}) copy-start(bf16[1,512,2048]{2,1,0:T(8,128)(2,1)} %param.19) | copy-start | bytes 6291460
  83.7 175.6 %all-gather.29.cloned.1.call-start = ((), (), s32[]{:S(2)}) async-start(), calls=%async_computation.26 | async-start | bytes 3145728 | tf_op jit(solution)/shard_map/all_gather | solution.py:138
  120.7 217.7 %all-gather.21.cloned.1.call-start = ((), (), s32[]{:S(2)}) async-start(), calls=%async_computation.13 | async-start | bytes 8912896 | tf_op jit(solution)/shard_map/all_gather | solution.py:99
  121.3 343.5 %all-gather.23.cloned.1.call-start = ((), (), s32[]{:S(2)}) async-start(), calls=%async_computation.14 | async-start | bytes 26738688 | tf_op jit(solution)/shard_map/all_gather | solution.py:164
  122.0 472.9 %all-gather.25.cloned.1.call-start = ((), (), s32[]{:S(2)}) async-start(), calls=%async_computation.15 | async-start | bytes 26738688 | tf_op jit(solution)/shard_map/all_gather | solution.py:165
  122.8 602.4 %all-gather.27.cloned.1.call-start = ((), (), s32[]{:S(2)}) async-start(), calls=%async_computation.16 | async-start | bytes 26738688 | tf_op jit(solution)/shard_map/all_gather | solution.py:166
  123.5 852.4 %reduce-scatter.10.cloned.1.call-start = ((), (), s32[]{:S(2)}) async-start(), calls=%async_computation.17 | async-start | bytes 3145728 | tf_op jit(solution)/shard_map/reduce_scatter | solution.py:242
  123.6 78.5 %copy-start.57 = (f32[128]{0:T(128)}, f32[128]{0:T(128)S(1)}, u32[]{:S(2)}) copy-start(f32[128]{0:T(128)S(1)} %convert_element_type.251) | copy-start | bytes 1540
  350.0 135.4 %copy-start.54 = (f32[512]{0:T(512)}, f32[512]{0:T(512)S(1)}, u32[]{:S(2)}) copy-start(f32[512]{0:T(512)S(1)} %get-tuple-element.365) | copy-start | bytes 6148
  352.5 242.4 %copy-start.24 = (bf16[512,2048]{1,0:T(8,128)(2,1)}, bf16[512,2048]{1,0:T(8,128)(2,1)S(1)}, u32[]{:S(2)}) copy-start(bf16[512,2048]{1,0:T(8,128)(2,1)S(1)} %multiply_convert_fusion.3) | copy-start | bytes 6291460
  776.7 21.4 copy-start.11
  776.7 21.4 copy-start.28
  943.9 66.8 %reduce-scatter.12.cloned.1.call-start = ((), (), s32[]{:S(2)}) async-start(), calls=%async_computation.18 | async-start | bytes 3145728 | tf_op jit(solution)/shard_map/reduce_scatter | solution.py:245
  944.7 187.4 %reduce-scatter.16.cloned.1.call-start = ((), (), s32[]{:S(2)}) async-start(), calls=%async_computation.20 | async-start | bytes 4456448 | tf_op jit(solution)/shard_map/reduce_scatter | solution.py:53
  998.1 164.6 %reduce-scatter.18.cloned.1.call-start = ((), (), s32[]{:S(2)}) async-start(), calls=%async_computation.21 | async-start | bytes 4456448 | tf_op jit(solution)/shard_map/reduce_scatter | solution.py:53
  1016.5 253.8 %reduce-scatter.14.cloned.1.call-start = ((), (), s32[]{:S(2)}) async-start(), calls=%async_computation.19 | async-start | bytes 8912896 | tf_op jit(solution)/shard_map/reduce_scatter | solution.py:53
  1057.8 320.8 %reduce-scatter.20.cloned.1.call-start = ((), (), s32[]{:S(2)}) async-start(), calls=%async_computation.22 | async-start | bytes 8912896 | tf_op jit(solution)/shard_map/reduce_scatter | solution.py:53
  1068.8 557.4 %reduce-scatter.22.cloned.1.call-start = ((), (), s32[]{:S(2)}) async-start(), calls=%async_computation.23 | async-start | bytes 26738688 | tf_op jit(solution)/shard_map/reduce_scatter | solution.py:53
  1090.0 783.3 %reduce-scatter.24.cloned.1.call-start = ((), (), s32[]{:S(2)}) async-start(), calls=%async_computation.24 | async-start | bytes 26738688 | tf_op jit(solution)/shard_map/reduce_scatter | solution.py:53
  1109.5 1010.7 %reduce-scatter.26.cloned.1.call-start = ((), (), s32[]{:S(2)}) async-start(), calls=%async_computation.25 | async-start | bytes 26738688 | tf_op jit(solution)/shard_map/reduce_scatter | solution.py:53
  1130.5 1147.3 %all-reduce.16.cloned.1.call-start = ((), (), s32[]{:S(2)}) async-start(), calls=%async_computation.27 | async-start | bytes 12582912 | tf_op jit(solution)/shard_map/psum | solution.py:272
  2120.2 21.4 copy-start.33
  2120.2 21.4 copy-start.64
  2150.6 79.4 %copy-start.50 = (f32[512]{0:T(512)S(1)}, f32[512]{0:T(512)}, u32[]{:S(2)}) copy-start(f32[512]{0:T(512)} %copy-done.49) | copy-start | bytes 6148
  (55 other events, 280.8 us)
Sparse Core Ops, SparseCore 0:
  10.2 53.6 all-gather.14
  66.0 49.0 all-gather.12
  117.3 73.4 all-gather.18
  192.8 31.3 all-gather.16
  226.1 33.1 all-gather.28
  261.3 74.9 all-gather.20
  337.9 126.8 all-gather.22
  466.3 128.5 all-gather.24
  596.6 128.5 all-gather.26
  944.1 31.8 reduce-scatter.9
  978.8 31.8 reduce-scatter.11
  1014.4 72.4 reduce-scatter.15
  1091.3 71.3 reduce-scatter.17
  1166.6 103.6 reduce-scatter.13
  1274.2 104.3 reduce-scatter.19
  1382.6 243.6 reduce-scatter.21
  1630.2 243.0 reduce-scatter.23
  1877.2 242.9 reduce-scatter.25
  2123.2 154.5 all-reduce.15
where the time goes:
time: 2310 us; the launch traced here: 2300 us
  waiting for transfers between devices  1540 us (67%)
  matrix products  405 us (18%)
  blocking collectives  138 us (6%)
  other arithmetic  94.6 us (4%)
  local copies, waits for them, and re-layouts  61.7 us (3%)
  loops' own time  42.4 us (2%)
    reduce_scatter x7, waiting for transfers between devices, shard_grad(): lax.psum_scatter(lax.dot_general(left, right, (((0,), (0,)), ((), ())), p...  988 us
    all_gather x1, waiting for transfers between devices, on_device(): lax.all_gather(w_gate, ('dp', 'fsdp'), axis=0, tiled=True)  112 us
    all_gather x1, waiting for transfers between devices, on_device(): lax.all_gather(w_down, ('dp', 'fsdp'), axis=0, tiled=True)  110 us
    all_gather x1, waiting for transfers between devices, on_device(): lax.all_gather(w_up, ('dp', 'fsdp'), axis=0, tiled=True)  109 us
    dot_general x7, matrix products, back_product(): lax.dot_general(left, right, (((1,), (1,)), ((), ())), preferred_element_...  103 us
    dot_general x7, matrix products, product(): return jnp.dot(left, right, preferred_element_type=jnp.float32)  92.3 us
    unnamed x2, blocking collectives  90.4 us
    dot_general x7, matrix products, shard_grad(): lax.dot_general(left, right, (((0,), (0,)), ((), ())), preferred_element_...  87 us
  transfers between devices with their start and end apart: 19, of which 16 were waited for; matrix products, arithmetic and copies ran while one was open for 15% of the time, Pallas kernels for 0%

commit v1 on v0

v1 whole, which is shorter than its diff:
```python
import functools

import jax
import jax.numpy as jnp
import numpy as np
from jax import lax
from jax.experimental import pallas as pl
from jax.experimental.pallas import tpu as pltpu
from jax.sharding import PartitionSpec as P

HEADS = 16
KV_HEADS = 8
HEAD_DIM = 128
GROUP = HEADS // KV_HEADS
HALF = HEAD_DIM // 2
EPS = 1e-06
THETA = 1000000.0
AXES = ("dp", "ctx", "fsdp")
BF = jnp.bfloat16
F32 = jnp.float32


def dot(left, right, dims=((1,), (0,))):
    return lax.dot_general(left, right, (dims, ((), ())), preferred_element_type=F32)


NT = ((1,), (1,))
TN = ((0,), (0,))


def to_natural(nat_ref, src, dst, block, blocks):
    for b in range(blocks):
        row = pl.multiple_of(nat_ref[b] * block, block)
        dst[pl.ds(row, block), :] = src[b * block : (b + 1) * block, :]


def from_natural(nat_ref, src, dst, block, blocks):
    for b in range(blocks):
        row = pl.multiple_of(nat_ref[b] * block, block)
        dst[b * block : (b + 1) * block, :] = src[pl.ds(row, block), :].astype(dst.dtype)


def unit(lin):
    scale = lax.rsqrt(jnp.mean(lin * lin, axis=-1, keepdims=True) + EPS)
    return lin * scale, scale


def rope(values, cosine, sine):
    return values * cosine + pltpu.roll(values, HALF, 1) * sine


def unrope(values, cosine, sine):
    return values * cosine + pltpu.roll(values * sine, HALF, 1)


def stack_heads(values):
    return jnp.concatenate(
        [values[:, i * HEAD_DIM : (i + 1) * HEAD_DIM] for i in range(GROUP)], axis=0
    )


def unstack_heads(values, rows):
    return jnp.concatenate([values[i * rows : (i + 1) * rows] for i in range(GROUP)], axis=1)


def softmax_tile(query, key, tile, i):
    scores = lax.dot_general(query, key, (NT, ((), ())), preferred_element_type=F32)
    width = (i + 1) * tile
    row = lax.broadcasted_iota(jnp.int32, (GROUP * tile, width), 0) % tile + i * tile
    col = lax.broadcasted_iota(jnp.int32, (GROUP * tile, width), 1)
    scores = jnp.where(col <= row, scores, -1e30)
    highest = jnp.max(scores, axis=-1, keepdims=True)
    exponent = jnp.exp(scores - highest)
    total = jnp.sum(exponent, axis=-1, keepdims=True)
    return exponent * (1.0 / total)


def prepare(lin_ref, cos_ref, sin_ref, gq_ref, gk_ref, nat_ref, q_nat, k_nat, v_nat, block, blocks):
    for b in range(blocks):
        row = pl.multiple_of(nat_ref[b] * block, block)
        rows = slice(b * block, (b + 1) * block)
        cosine, sine = cos_ref[rows, :], sin_ref[rows, :]
        for i in range(GROUP):
            cols = slice(i * HEAD_DIM, (i + 1) * HEAD_DIM)
            normed, _ = unit(lin_ref[rows, cols])
            q_nat[pl.ds(row, block), cols] = (
                rope(normed * gq_ref[...], cosine, sine) * HEAD_DIM**-0.5
            ).astype(BF)
        cols = slice(GROUP * HEAD_DIM, (GROUP + 1) * HEAD_DIM)
        normed, _ = unit(lin_ref[rows, cols])
        k_nat[pl.ds(row, block), :] = rope(normed * gk_ref[...], cosine, sine).astype(BF)
        cols = slice((GROUP + 1) * HEAD_DIM, (GROUP + 2) * HEAD_DIM)
        v_nat[pl.ds(row, block), :] = lin_ref[rows, cols].astype(BF)


def attend_kernel(
    block, blocks, tile, nat_ref, lin_ref, cos_ref, sin_ref, gq_ref, gk_ref, o_ref, q_nat, k_nat, v_nat, o_nat
):
    prepare(lin_ref, cos_ref, sin_ref, gq_ref, gk_ref, nat_ref, q_nat, k_nat, v_nat, block, blocks)
    for i in range(blocks * block // tile):
        width = (i + 1) * tile
        rows = slice(i * tile, width)
        probs = softmax_tile(stack_heads(q_nat[rows, :]), k_nat[:width, :], tile, i).astype(BF)
        out = jnp.dot(probs, v_nat[:width, :], preferred_element_type=F32)
        o_nat[rows, :] = unstack_heads(out, tile).astype(BF)
    from_natural(nat_ref, o_nat, o_ref, block, blocks)


def attend_back_kernel(
    block, blocks, tile, nat_ref, lin_ref, do_ref, cos_ref, sin_ref, gq_ref, gk_ref,
    d_ref, dgq_ref, dgk_ref, q_nat, k_nat, v_nat, do_nat, dq_nat, dk_nat, dv_nat
):
    @pl.when((pl.program_id(0) == 0) & (pl.program_id(1) == 0))
    def _():
        dgq_ref[...] = jnp.zeros_like(dgq_ref)
        dgk_ref[...] = jnp.zeros_like(dgk_ref)

    prepare(lin_ref, cos_ref, sin_ref, gq_ref, gk_ref, nat_ref, q_nat, k_nat, v_nat, block, blocks)
    to_natural(nat_ref, do_ref, do_nat, block, blocks)
    tiles = blocks * block // tile
    for i in reversed(range(tiles)):
        width = (i + 1) * tile
        rows = slice(i * tile, width)
        query, key, value = stack_heads(q_nat[rows, :]), k_nat[:width, :], v_nat[:width, :]
        grad = stack_heads(do_nat[rows, :])
        probs = softmax_tile(query, key, tile, i)
        d_probs = lax.dot_general(grad, value, (NT, ((), ())), preferred_element_type=F32)
        inner = jnp.sum(d_probs * probs, axis=-1, keepdims=True)
        d_scores = (probs * (d_probs - inner)).astype(BF)
        d_query = jnp.dot(d_scores, key, preferred_element_type=F32)
        dq_nat[rows, :] = unstack_heads(d_query, tile)
        d_key = lax.dot_general(d_scores, query, (TN, ((), ())), preferred_element_type=F32)
        d_value = lax.dot_general(
            probs.astype(BF), grad, (TN, ((), ())), preferred_element_type=F32
        )
        if i == tiles - 1:
            dk_nat[...] = d_key
            dv_nat[...] = d_value
        else:
            dk_nat[:width, :] += d_key
            dv_nat[:width, :] += d_value
    for b in range(blocks):
        row = pl.multiple_of(nat_ref[b] * block, block)
        rows = slice(b * block, (b + 1) * block)
        cosine, sine = cos_ref[rows, :], sin_ref[rows, :]
        for i in range(GROUP + 1):
            cols = slice(i * HEAD_DIM, (i + 1) * HEAD_DIM)
            normed, scale = unit(lin_ref[rows, cols])
            if i < GROUP:
                grad = unrope(dq_nat[pl.ds(row, block), cols] * HEAD_DIM**-0.5, cosine, sine)
                gain_ref, total_ref = gq_ref, dgq_ref
            else:
                grad = unrope(dk_nat[pl.ds(row, block), :], cosine, sine)
                gain_ref, total_ref = gk_ref, dgk_ref
            total_ref[0:1, :] += jnp.sum(grad * normed, axis=0, keepdims=True)
            grad = grad * gain_ref[...]
            grad = scale * (grad - normed * jnp.mean(grad * normed, axis=-1, keepdims=True))
            d_ref[rows, cols] = grad.astype(BF)
        cols = slice((GROUP + 1) * HEAD_DIM, (GROUP + 2) * HEAD_DIM)
        d_ref[rows, cols] = dv_nat[pl.ds(row, block), :].astype(BF)


VMEM_LIMIT = 56 * 1024 * 1024


def attend(lin, cosine, sine, gq, gk, nat, seqs, heads, block):
    tokens = lin.shape[0]
    length = tokens // seqs
    blocks = length // block
    tile = min(256, length)
    width = (GROUP + 2) * HEAD_DIM
    table = pl.BlockSpec((length, HEAD_DIM), lambda s, h, n: (s, 0))
    gain = pl.BlockSpec((1, HEAD_DIM), lambda s, h, n: (0, 0))
    work = seqs * heads * GROUP * length * length * HEAD_DIM
    return pl.pallas_call(
        functools.partial(attend_kernel, block, blocks, tile),
        grid_spec=pltpu.PrefetchScalarGridSpec(
            num_scalar_prefetch=1,
            grid=(seqs, heads),
            in_specs=[pl.BlockSpec((length, width), lambda s, h, n: (s, h)), table, table, gain, gain],
            out_specs=pl.BlockSpec((length, GROUP * HEAD_DIM), lambda s, h, n: (s, h)),
            scratch_shapes=[
                pltpu.VMEM((length, GROUP * HEAD_DIM), BF),
                pltpu.VMEM((length, HEAD_DIM), BF),
                pltpu.VMEM((length, HEAD_DIM), BF),
                pltpu.VMEM((length, GROUP * HEAD_DIM), BF),
            ],
        ),
        out_shape=jax.ShapeDtypeStruct((tokens, heads * GROUP * HEAD_DIM), BF),
        compiler_params=pltpu.CompilerParams(vmem_limit_bytes=VMEM_LIMIT),
        cost_estimate=pl.CostEstimate(
            flops=3 * work, bytes_accessed=lin.size * 4, transcendentals=work // HEAD_DIM
        ),
        name="attend",
    )(nat, lin, cosine, sine, gq, gk)


def attend_back(lin, d_out, cosine, sine, gq, gk, nat, seqs, heads, block):
    tokens = lin.shape[0]
    length = tokens // seqs
    blocks = length // block
    tile = min(256, length)
    width = (GROUP + 2) * HEAD_DIM
    table = pl.BlockSpec((length, HEAD_DIM), lambda s, h, n: (s, 0))
    gain = pl.BlockSpec((1, HEAD_DIM), lambda s, h, n: (0, 0))
    total = pl.BlockSpec((8, HEAD_DIM), lambda s, h, n: (0, 0))
    work = seqs * heads * GROUP * length * length * HEAD_DIM
    return pl.pallas_call(
        functools.partial(attend_back_kernel, block, blocks, tile),
        grid_spec=pltpu.PrefetchScalarGridSpec(
            num_scalar_prefetch=1,
            grid=(seqs, heads),
            in_specs=[
                pl.BlockSpec((length, width), lambda s, h, n: (s, h)),
                pl.BlockSpec((length, GROUP * HEAD_DIM), lambda s, h, n: (s, h)),
                table, table, gain, gain,
            ],
            out_specs=[pl.BlockSpec((length, width), lambda s, h, n: (s, h)), total, total],
            scratch_shapes=[
                pltpu.VMEM((length, GROUP * HEAD_DIM), BF),
                pltpu.VMEM((length, HEAD_DIM), BF),
                pltpu.VMEM((length, HEAD_DIM), BF),
                pltpu.VMEM((length, GROUP * HEAD_DIM), BF),
                pltpu.VMEM((length, GROUP * HEAD_DIM), F32),
                pltpu.VMEM((length, HEAD_DIM), F32),
                pltpu.VMEM((length, HEAD_DIM), F32),
            ],
        ),
        out_shape=[
            jax.ShapeDtypeStruct((tokens, heads * width), BF),
            jax.ShapeDtypeStruct((8, HEAD_DIM), F32),
            jax.ShapeDtypeStruct((8, HEAD_DIM), F32),
        ],
        compiler_params=pltpu.CompilerParams(vmem_limit_bytes=VMEM_LIMIT),
        cost_estimate=pl.CostEstimate(
            flops=7 * work, bytes_accessed=lin.size * 8, transcendentals=work // HEAD_DIM
        ),
        name="attend_back",
    )(nat, lin, d_out, cosine, sine, gq, gk)


class Grid:
    def __init__(self, mesh):
        self.Z, self.Y, self.F = (mesh.shape[n] for n in AXES)
        self.C = 2 if self.F % 2 == 0 and KV_HEADS % (2 * self.Y) == 0 else 1
        self.A = self.F // self.C
        self.T = self.Y * self.C
        self.ZA = self.Z * self.A
        self.shape = (self.Z, self.Y, self.A, self.C)

    def index(self):
        f = lax.axis_index("fsdp")
        return lax.axis_index("dp"), lax.axis_index("ctx"), f // self.C, f % self.C

    def permute(self, value, target):
        pairs = []
        for i in range(int(np.prod(self.shape))):
            at = np.unravel_index(i, self.shape)
            pairs.append((i, int(np.ravel_multi_index(target(*(int(k) for k in at)), self.shape))))
        return lax.ppermute(value, AXES, pairs)

    def send(self, value, z=0, y=0, a=0, c=0):
        return self.permute(
            value,
            lambda i, j, k, l: ((i + z) % self.Z, (j + y) % self.Y, (k + a) % self.A, (l + c) % self.C),
        )


def on_device(
    grid, tokens, cotangent, positions, block_map, w_query, w_key, w_value, w_output, w_gate, w_up, w_down,
    gain_attn, gain_mlp, gain_query, gain_key,
):
    Z, Y, A, C, T, ZA = grid.Z, grid.Y, grid.A, grid.C, grid.T, grid.ZA
    send = grid.send
    z, y, a, c = grid.index()
    seq_count, local_rows, width = tokens.shape
    rows = seq_count * local_rows
    block = local_rows // 2
    group_tokens = T * rows
    seqs = C * seq_count
    hidden_units = w_gate.shape[1]
    heads = KV_HEADS // T

    def gather_tokens(own):
        chunks = [None] * Y
        chunks[0] = held = own
        for k in range(1, Y):
            held = send(held, y=1)
            chunks[Y - k] = held
        parts = list(chunks)
        if C == 2:
            parts += [send(chunk, c=1) for chunk in chunks]
        return jnp.concatenate(parts, axis=0)

    def scatter_tokens(partial):
        parts = partial.reshape(C, Y, rows, width)
        if C == 2:
            other = [send(parts[1, j], c=1) for j in range(Y)]
            summed = [parts[0, j].astype(F32) + other[j].astype(F32) for j in range(Y)]
        else:
            summed = [parts[0, j].astype(F32) for j in range(Y)]
        total = summed[Y - 1]
        for k in range(1, Y):
            total = send(total.astype(BF), y=1).astype(F32) + summed[Y - 1 - k]
        return total

    def gather_blocks(own):
        buffer = jnp.zeros((Z, A) + own.shape, own.dtype)
        held = own
        for s in range(Z):
            if s:
                held = send(held, z=1)
            piece = held
            for k in range(A):
                if k:
                    piece = send(piece, a=1)
                buffer = lax.dynamic_update_slice(
                    buffer, piece[None, None], ((z - s) % Z, (a - k) % A) + (0,) * own.ndim
                )
        return buffer

    def scatter_blocks(partial):
        def term(i, j):
            at = ((z + i) % Z, (a + j) % A) + (0,) * (partial.ndim - 2)
            return lax.dynamic_slice(partial, at, (1, 1) + partial.shape[2:])[0, 0].astype(F32)

        def over_a(i):
            total = term(i, A - 1)
            for k in range(1, A):
                total = send(total.astype(BF), a=1).astype(F32) + term(i, A - 1 - k)
            return total

        total = over_a(Z - 1)
        for s in range(1, Z):
            total = send(total.astype(BF), z=1).astype(F32) + over_a(Z - 1 - s)
        return total

    def own_columns(shard):
        own = lax.dynamic_slice_in_dim(shard, y * C + c, 1, 1)[:, 0]
        if C == 1:
            return own
        other = send(lax.dynamic_slice_in_dim(shard, y * C + (1 - c), 1, 1)[:, 0], c=1)
        return jnp.concatenate([jnp.where(c == 0, own, other), jnp.where(c == 0, other, own)], axis=0)

    def shard_of_columns(total):
        total = total.astype(BF)
        if C == 2:
            pair = total.reshape(2, -1, total.shape[-1])
            own = lax.dynamic_index_in_dim(pair, c, 0, keepdims=False)
            other = send(lax.dynamic_index_in_dim(pair, 1 - c, 0, keepdims=False), c=1)
            own = jnp.stack([jnp.where(c == 0, own, other), jnp.where(c == 0, other, own)], axis=1)
        else:
            own = total[:, None]
        whole = jnp.zeros((own.shape[0], Y) + own.shape[1:], F32)
        held = own
        for k in range(Y):
            if k:
                held = send(held, y=1)
            whole = lax.dynamic_update_slice(
                whole, held[:, None].astype(F32), (0, (y - k) % Y, 0, 0)
            )
        return whole

    shard_rows = w_query.shape[0]
    pack = jnp.concatenate([gain_attn, gain_mlp, gain_query, gain_key])
    qkv_width = (GROUP + 2) * HEAD_DIM * KV_HEADS // T
    pack = jnp.pad(pack, (0, qkv_width * 8 - pack.shape[0])).reshape(8, 1, qkv_width)
    qkv_shard = jnp.concatenate(
        [
            w_query.reshape(shard_rows, KV_HEADS, GROUP * HEAD_DIM),
            w_key.reshape(shard_rows, KV_HEADS, HEAD_DIM),
            w_value.reshape(shard_rows, KV_HEADS, HEAD_DIM),
        ],
        axis=2,
    ).reshape(shard_rows, T, qkv_width)
    qkv_shard = jnp.concatenate([qkv_shard, jnp.broadcast_to(pack, (8, T, qkv_width))], axis=0)

    x_group = gather_tokens(tokens.reshape(rows, width))
    place = gather_tokens(positions.reshape(rows, 1))[:, 0]

    qkv_all = gather_blocks(own_columns(qkv_shard)).reshape(ZA * C, shard_rows + 8, qkv_width)
    w_qkv = qkv_all[:, :shard_rows].reshape(width, qkv_width)
    packs = qkv_all[:, shard_rows:].reshape(ZA * C, -1)
    n, m = gain_attn.shape[0], gain_query.shape[0]
    ga = packs[:, :n].reshape(1, width).astype(F32)
    gm = packs[:, n : 2 * n].reshape(1, width).astype(F32)
    gq = packs[:, 2 * n : 2 * n + m].reshape(1, HEAD_DIM).astype(F32)
    gk = packs[:, 2 * n + m : 2 * n + 2 * m].reshape(1, HEAD_DIM).astype(F32)

    def out_target(i, j, k, l):
        b = ((i * A + k) * C + l) * Y + j
        rank, at = b // ZA, b % ZA
        return (at // A, rank // C, at % A, rank % C)

    def out_source(i, j, k, l):
        b = (j * C + l) * ZA + i * A + k
        shard, copy = b // Y, b % Y
        return (shard // C // A, copy, shard // C % A, shard % C)

    out_rows = w_output.shape[0] // Y
    wo_block = grid.permute(lax.dynamic_slice_in_dim(w_output, y * out_rows, out_rows, 0), out_target)
    w_out = gather_blocks(wo_block).reshape(-1, width)

    down_rows = w_down.shape[0] // Y

    def hidden_columns(shard):
        split = shard.reshape(shard.shape[0], ZA, C, Y, down_rows)
        return split.transpose(0, 3, 2, 1, 4).reshape(shard.shape[0], T, ZA * down_rows)

    w_g = gather_blocks(own_columns(hidden_columns(w_gate))).reshape(width, -1)
    w_u = gather_blocks(own_columns(hidden_columns(w_up))).reshape(width, -1)
    w_d = gather_blocks(lax.dynamic_slice_in_dim(w_down, y * down_rows, down_rows, 0)).reshape(-1, width)

    freqs = THETA ** (-(jnp.arange(HALF, dtype=F32) * 2.0 / HEAD_DIM))
    angles = place.astype(F32)[:, None] * freqs
    cosine, sine = jnp.cos(angles), jnp.sin(angles)
    cosine = jnp.concatenate([cosine, cosine], axis=1)
    sine = jnp.concatenate([-sine, sine], axis=1)
    order = (jnp.arange(Y, dtype=jnp.int32) + y) % Y
    nat = jnp.take(block_map.reshape(Y, 2), order, axis=0).reshape(-1)

    def unit_rows(values):
        scale = lax.rsqrt(jnp.mean(values * values, axis=-1, keepdims=True) + EPS)
        return values * scale, scale

    def norm_back(grad, gain, normed, scale):
        grad = grad * gain
        return scale * (grad - normed * jnp.mean(grad * normed, axis=-1, keepdims=True))

    x_unit, _ = unit_rows(x_group.astype(F32))
    h1 = (x_unit * ga).astype(BF)
    lin = dot(h1, w_qkv)
    attended = attend(lin, cosine, sine, gq, gk, nat, seqs, heads, block)
    x_own = tokens.reshape(rows, width).astype(F32)
    x_mid = x_own + scatter_tokens(dot(attended, w_out).astype(BF))

    mid_unit, mid_scale = unit_rows(x_mid)
    h2 = gather_tokens((mid_unit * gm).astype(BF))
    dy = gather_tokens(cotangent.reshape(rows, width))
    gate = dot(h2, w_g)
    upper = dot(h2, w_u)
    sigmoid = 1.0 / (1.0 + jnp.exp(-gate))
    silu = gate * sigmoid
    hidden = (silu * upper).astype(BF)
    gate_factor = (upper * sigmoid * (1.0 + gate * (1.0 - sigmoid))).astype(BF)
    upper_factor = silu.astype(BF)
    grad_down = dot(hidden, dy, TN).astype(BF)
    output = x_mid + scatter_tokens(dot(hidden, w_d).astype(BF))
    d_hidden = dot(dy, w_d, NT)
    d_gate = (d_hidden * gate_factor.astype(F32)).astype(BF)
    d_upper = (d_hidden * upper_factor.astype(F32)).astype(BF)
    d_h2 = scatter_tokens((dot(d_gate, w_g, NT) + dot(d_upper, w_u, NT)).astype(BF))
    grad_gate = dot(h2, d_gate, TN).astype(BF)
    grad_up = dot(h2, d_upper, TN).astype(BF)
    sum_mlp = jnp.sum(d_h2 * mid_unit, axis=0)
    d_mid = cotangent.reshape(rows, width).astype(F32) + norm_back(d_h2, gm, mid_unit, mid_scale)

    d_branch = gather_tokens(d_mid.astype(BF))
    d_attended = dot(d_branch, w_out, NT).astype(BF)
    grad_output = dot(attended, d_branch, TN).astype(BF)
    d_lin, sum_query, sum_key = attend_back(
        lin, d_attended, cosine, sine, gq, gk, nat, seqs, heads, block
    )
    grad_qkv = dot(h1, d_lin, TN).astype(BF)
    d_h1_part = dot(d_lin, w_qkv, NT)
    sum_attn = jnp.sum(d_h1_part * x_unit, axis=0)
    d_h1 = scatter_tokens(d_h1_part.astype(BF))
    own_unit, own_scale = unit_rows(x_own)
    grad_tokens = d_mid + norm_back(d_h1, ga, own_unit, own_scale)

    def columns_grad(partial):
        return shard_of_columns(scatter_blocks(partial.reshape(Z, A, -1, partial.shape[-1])))

    def hidden_grad(partial):
        whole = columns_grad(partial).reshape(shard_rows, Y, C, ZA, down_rows)
        return whole.transpose(0, 3, 2, 1, 4).reshape(shard_rows, hidden_units)

    def y_copies(own):
        whole = jnp.zeros((Y,) + own.shape, F32)
        held = own.astype(BF)
        for k in range(Y):
            if k:
                held = send(held, y=1)
            whole = lax.dynamic_update_slice(whole, held[None].astype(F32), ((y - k) % Y, 0, 0))
        return whole.reshape(-1, own.shape[-1])

    g_down = y_copies(scatter_blocks(grad_down.reshape(Z, A, down_rows, width)))
    g_gate = hidden_grad(grad_gate)
    g_up = hidden_grad(grad_up)
    g_out = scatter_blocks(grad_output.reshape(Z, A, -1, width)).astype(BF)
    g_out = y_copies(grid.permute(g_out, out_source))
    g_qkv = columns_grad(grad_qkv).reshape(shard_rows, KV_HEADS, (GROUP + 2) * HEAD_DIM)
    g_query = g_qkv[:, :, : GROUP * HEAD_DIM].reshape(shard_rows, -1)
    g_key = g_qkv[:, :, GROUP * HEAD_DIM : (GROUP + 1) * HEAD_DIM].reshape(shard_rows, -1)
    g_value = g_qkv[:, :, (GROUP + 1) * HEAD_DIM :].reshape(shard_rows, -1)

    sums = lax.psum(
        jnp.concatenate([sum_attn, sum_mlp, sum_query[0], sum_key[0]]), AXES
    )
    shard = (z * A + a) * C + c
    s_attn = lax.dynamic_slice_in_dim(sums, shard * n, n)
    s_mlp = lax.dynamic_slice_in_dim(sums, width + shard * n, n)
    s_query = lax.dynamic_slice_in_dim(sums, 2 * width + shard * m, m)
    s_key = lax.dynamic_slice_in_dim(sums, 2 * width + HEAD_DIM + shard * m, m)
    return (
        output.astype(BF).reshape(tokens.shape), grad_tokens.astype(BF).reshape(tokens.shape),
        g_query, g_key, g_value, g_out, g_gate, g_up, g_down, s_attn, s_mlp, s_query, s_key,
    )


def solution(mesh):
    sharded = P(("dp", "fsdp"), None)
    vector = P(("dp", "fsdp"))
    tokens = P(("dp", "fsdp"), "ctx", None)
    return jax.shard_map(
        functools.partial(on_device, Grid(mesh)),
        mesh=mesh,
        in_specs=(tokens, tokens, P(("dp", "fsdp"), "ctx"), P()) + (sharded,) * 7 + (vector,) * 4,
        out_specs=(tokens, tokens) + (sharded,) * 7 + (vector,) * 4,
        check_vma=False,
    )
```

time: 2310 us -> 1230 us (0.53)
  waiting for transfers between devices: 1540 us -> 530 us
  matrix products: 405 us -> 254 us
  starting transfers between devices: 1.55 us -> 96.8 us
  blocking collectives: 138 us -> 43.5 us
  local copies, waits for them, and re-layouts: 61.7 us -> 144 us
  Pallas kernels: 0 us -> 57.6 us
  loops' own time: 42.4 us -> 0 us
    reduce_scatter x9 -> x0, waiting for transfers between devices: 1030 us -> none  [the longest x7 988 us: shard_grad(): lax.psum_scatter(lax.dot_general(left, right, (((0,), (0,)), ((), ())), p...]
    ppermute x0 -> x110, waiting for transfers between devices: none -> 530 us  [permute(): return lax.ppermute(value, AXES, pairs)]
    all_gather x9 -> x0, waiting for transfers between devices: 457 us -> none  [the longest x1 112 us: on_device(): lax.all_gather(w_gate, ('dp', 'fsdp'), axis=0, tiled=True)]
    dot_general x77 -> x15, matrix products: 405 us -> 254 us  [dot(): lax.dot_general(left, right, (dims, ((), ())), preferred_element_type=F32)]
    ppermute x0 -> x110, starting transfers between devices: none -> 96.8 us  [permute(): return lax.ppermute(value, AXES, pairs)]
    unnamed x2 -> x0, blocking collectives: 90.4 us -> none
    pallas_call x0 -> x2, Pallas kernels: none -> 57.6 us  [the longest x1 36.8 us: attend_back(): pl.pallas_call(functools.partial(attend_back_kernel, block, blocks, tile)...]
    another operation x2 -> x0, loops' own time: 42.4 us -> none  [the longest x1 21.3 us: on_device(): outs_heads, log_totals = lax.map(attend, jnp.arange(KV_HEADS))]
  transfers between devices with their start and end apart: 19 -> 110, of which waited for: 16 -> 50; matrix products, arithmetic and copies ran while one was open for 15% -> 32% of each run, Pallas kernels for 0% -> 2%
where the time goes in v1:
time: 1230 us; the launch traced here: 1210 us
  waiting for transfers between devices  530 us (43%)
  matrix products  254 us (21%)
  local copies, waits for them, and re-layouts  144 us (12%)
  starting transfers between devices  96.8 us (8%)
  other arithmetic  87.3 us (7%)
  Pallas kernels  57.6 us (5%)
  blocking collectives  43.5 us (4%)
    ppermute x110, waiting for transfers between devices, permute(): return lax.ppermute(value, AXES, pairs)  530 us
    dot_general x15, matrix products, dot(): lax.dot_general(left, right, (dims, ((), ())), preferred_element_type=F32)  254 us
    ppermute x110, starting transfers between devices, permute(): return lax.ppermute(value, AXES, pairs)  96.8 us
    psum x1, blocking collectives, on_device(): lax.psum(jnp.concatenate([sum_attn, sum_mlp, sum_query[0], sum_key[0]]),...  43.5 us
    pallas_call x1, Pallas kernels, attend_back(): pl.pallas_call(functools.partial(attend_back_kernel, block, blocks, tile)...  36.8 us
    unnamed x135, local copies, waits for them, and re-layouts  36.1 us
    dynamic_update_slice x37, local copies, waits for them, and re-layouts, gather_blocks(): lax.dynamic_update_slice(buffer, piece[None, None], ((z - s) % Z, (a - k)...  24.6 us
  transfers between devices with their start and end apart: 110, of which 50 were waited for; matrix products, arithmetic and copies ran while one was open for 32% of the time, Pallas kernels for 2%

profile of v1, /device:TPU:0, one launch (start us, length us, event | category | flops | bytes accessed | tf_op | source)
XLA Modules:
  0.0 1215.0 jit_solution(16370010681277371261)
XLA Ops:
  25.1 24.6 %collective-permute-done.11 = s32[512,1]{0,1:T(1,128)S(1)} collective-permute-done((s32[512,1]{0,1:T(1,128)}, s32[512,1]{0,1:T(1,128)S(1)}, u32[]{:S(2)}, u32[]{:S(2)}) %collective-permute-start.11) | collective-permute-done | bytes 2080 | tf_op jit(solution)/shard_map/ppermute | solution.py:260
  171.3 13.3 %collective-permute-done.10 = bf16[272,1024]{1,0:T(8,128)(2,1)S(1)} collective-permute-done((bf16[272,1024]{1,0:T(8,128)(2,1)S(1)}, bf16[272,1024]{1,0:T(8,128)(2,1)S(1)}, u32[]{:S(2)}, u32[]{:S(2)}) %collective-permute-start.10) | collective-permute-done | bytes 557088 | tf_op jit(solution)/shard_map/ppermute | solution.py:260
  196.1 15.8 %fusion.26.lin_ref = f32[2048,1024]{1,0:T(8,128)} fusion(bf16[2048,1024]{1,0:T(8,128)(2,1)S(1)} %bitcast.487, f32[2048]{0:T(1024)S(1)} %get-tuple-element.130, f32[2048]{0:T(1024)S(1)} %add_rsqrt_fusion, bf16[512,2048]{1,0:T(8,128)(2,1)} %collective-permute-done.2, bf16[512,2048]{1,0:T(8,128)(2,1)} %collective-permute-done.1, ...), kind=kOutput, calls=%fused_computation.64 | convolution fusion | flops 8636071936 | bytes 20987904 | tf_op jit(solution)/shard_map/dot_general | solution.py:24
  211.9 20.8 %attend.1 = bf16[2048,512]{1,0:T(8,128)(2,1)} custom-call(s32[4]{0:T(128)} %select_n.715.nat_ref, f32[2048,1024]{1,0:T(8,128)} %fusion.26.lin_ref, f32[2048,128]{1,0:T(8,128)} %get-tuple-element.143.cos_ref, f32[2048,128]{1,0:T(8,128)} %get-tuple-element.144.sin_ref, f32[1,128]{1,0:T(1,128)} %reshape.538.gq_ref, f32[1,128]{1,0:T(1,128)} %reshape.539.gk_ref), custom_call_target="tpu_custom_call" | custom-call | flops 3221225472 | bytes 8388608 | tf_op jit(solution)/shard_map/attend/pallas_call | solution.py:175
  249.1 13.3 %collective-permute-done.46 = bf16[192,2048]{1,0:T(8,128)(2,1)S(1)} collective-permute-done((bf16[192,2048]{1,0:T(8,128)(2,1)S(1)}, bf16[192,2048]{1,0:T(8,128)(2,1)S(1)}, u32[]{:S(2)}, u32[]{:S(2)}) %collective-permute-start.46) | collective-permute-done | bytes 786464 | tf_op jit(solution)/shard_map/ppermute | solution.py:260
  284.7 13.4 %collective-permute-done.31 = bf16[256,1536]{1,0:T(8,128)(2,1)S(1)} collective-permute-done((bf16[256,1536]{1,0:T(8,128)(2,1)S(1)}, bf16[256,1536]{1,0:T(8,128)(2,1)S(1)}, u32[]{:S(2)}, u32[]{:S(2)}) %collective-permute-start.31) | collective-permute-done | bytes 786464 | tf_op jit(solution)/shard_map/ppermute | solution.py:260
  371.3 14.7 %collective-permute-done.43 = bf16[256,1536]{1,0:T(8,128)(2,1)S(1)} collective-permute-done((bf16[256,1536]{1,0:T(8,128)(2,1)S(1)}, bf16[256,1536]{1,0:T(8,128)(2,1)S(1)}, u32[]{:S(2)}, u32[]{:S(2)}) %collective-permute-start.43) | collective-permute-done | bytes 786464 | tf_op jit(solution)/shard_map/ppermute | solution.py:260
  386.9 13.7 %collective-permute-done.35 = bf16[256,1536]{1,0:T(8,128)(2,1)S(1)} collective-permute-done((bf16[256,1536]{1,0:T(8,128)(2,1)S(1)}, bf16[256,1536]{1,0:T(8,128)(2,1)S(1)}, u32[]{:S(2)}, u32[]{:S(2)}) %collective-permute-start.35) | collective-permute-done | bytes 786464 | tf_op jit(solution)/shard_map/ppermute | solution.py:260
  404.8 21.9 %fusion.97 = f32[2048,1536]{1,0:T(8,128)} fusion(bf16[2048,1536]{1,0:T(8,128)(2,1)} %bitcast.66, bf16[512,2048]{1,0:T(8,128)(2,1)} %copy-done.56, bf16[512,2048]{1,0:T(8,128)(2,1)} %copy-done.55, bf16[512,2048]{1,0:T(8,128)(2,1)} %copy-done.52, bf16[512,2048]{1,0:T(8,128)(2,1)S(1)} %multiply_convert_fusion.4), kind=kOutput, calls=%fused_computation.306 | convolution fusion | flops 12918456320 | bytes 27262976 | tf_op jit(solution)/shard_map/dot_general | solution.py:24
  426.6 22.8 %fusion.98 = f32[2048,1536]{1,0:T(8,128)} fusion(bf16[2048,1536]{1,0:T(8,128)(2,1)} %bitcast.52, bf16[512,2048]{1,0:T(8,128)(2,1)} %copy-done.56, bf16[512,2048]{1,0:T(8,128)(2,1)} %copy-done.55, bf16[512,2048]{1,0:T(8,128)(2,1)S(1)} %copy-done.53, bf16[512,2048]{1,0:T(8,128)(2,1)S(1)} %multiply_convert_fusion.4), kind=kOutput, calls=%fused_computation.307 | convolution fusion | flops 12918456320 | bytes 27262976 | tf_op jit(solution)/shard_map/dot_general | solution.py:24
  449.4 29.8 %multiply_convert_fusion.1 = (bf16[2048,1536]{1,0:T(8,128)(2,1)}, bf16[2048,1536]{1,0:T(8,128)(2,1)}, bf16[2048,1536]{1,0:T(8,128)(2,1)}) fusion(f32[2048,1536]{1,0:T(8,128)} %fusion.98, f32[2048,1536]{1,0:T(8,128)} %fusion.97, bf16[1536,2048]{1,0:T(8,128)(2,1)} %bitcast.75, bf16[512,2048]{1,0:T(8,128)(2,1)} %collective-permute-done.56, ...), kind=kOutput, calls=%fused_computation.10 | convolution fusion | flops 12978225152 | bytes 58720256 | tf_op jit(solution)/shard_map/dot_general | solution.py:24
  479.3 17.1 %convolution_convert_fusion = bf16[2048,2048]{1,0:T(8,128)(2,1)S(1)} fusion(bf16[2048,1536]{1,0:T(8,128)(2,1)} %get-tuple-element.69, bf16[1536,2048]{1,0:T(8,128)(2,1)} %bitcast.75), kind=kOutput, calls=%fused_computation.19 | convolution fusion | flops 12889096192 | bytes 20971520 | tf_op jit(solution)/shard_map/dot_general | solution.py:24
  503.6 19.0 %fusion.104 = f32[2048,2048]{1,0:T(8,128)} fusion(bf16[2048,1536]{1,0:T(8,128)(2,1)S(1)} %copy-done.59, bf16[2048,1536]{1,0:T(8,128)(2,1)} %bitcast.66), kind=kOutput, calls=%fused_computation.312 | convolution fusion | flops 12884901888 | bytes 29360128 | tf_op jit(solution)/shard_map/dot_general | solution.py:24
  522.6 17.8 %convolution_convert_fusion.2 = bf16[1536,2048]{1,0:T(8,128)(2,1)S(1)} fusion(bf16[2048,1536]{1,0:T(8,128)(2,1)} %get-tuple-element.69, bf16[512,2048]{1,0:T(8,128)(2,1)} %collective-permute-done.56, bf16[512,2048]{1,0:T(8,128)(2,1)} %collective-permute-done.55, bf16[512,2048]{1,0:T(8,128)(2,1)} %collective-permute-done.54, bf16[512,2048]{1,0:T(8,128)(2,1)} %bitcast.82), kind=kOutput, calls=%fused_computation.21 | convolution fusion | flops 12921602048 | bytes 20971520 | tf_op jit(solution)/shard_map/dot_general | solution.py:24
  545.4 17.2 %convolution_convert_fusion.3 = bf16[2048,1536]{1,0:T(8,128)(2,1)S(1)} fusion(bf16[2048,1536]{1,0:T(8,128)(2,1)} %get-tuple-element.70, bf16[512,2048]{1,0:T(8,128)(2,1)} %copy-done.56, bf16[512,2048]{1,0:T(8,128)(2,1)} %copy-done.55, bf16[512,2048]{1,0:T(8,128)(2,1)S(1)} %copy-done.54, bf16[512,2048]{1,0:T(8,128)(2,1)S(1)} %multiply_convert_fusion.4), kind=kOutput, calls=%fused_computation.22 | convolution fusion | flops 12921602048 | bytes 20971520 | tf_op jit(solution)/shard_map/dot_general | solution.py:24
  569.0 21.6 %add_convert_fusion = bf16[2048,2048]{1,0:T(8,128)(2,1)} fusion(f32[2048,2048]{1,0:T(8,128)} %fusion.104, bf16[2048,1536]{1,0:T(8,128)(2,1)} %get-tuple-element.68, bf16[2048,1536]{1,0:T(8,128)(2,1)} %bitcast.52), kind=kOutput, calls=%fused_computation.8 | convolution fusion | flops 12893290496 | bytes 37748736 | tf_op jit(solution)/shard_map/dot_general | solution.py:24
  590.6 19.4 %convolution_convert_fusion.4 = bf16[2048,1536]{1,0:T(8,128)(2,1)} fusion(bf16[2048,1536]{1,0:T(8,128)(2,1)} %get-tuple-element.68, bf16[512,2048]{1,0:T(8,128)(2,1)} %copy-done.56, bf16[512,2048]{1,0:T(8,128)(2,1)} %copy-done.55, bf16[512,2048]{1,0:T(8,128)(2,1)} %copy-done.52, bf16[512,2048]{1,0:T(8,128)(2,1)S(1)} %multiply_convert_fusion.4), kind=kOutput, calls=%fused_computation.23 | convolution fusion | flops 12921602048 | bytes 20971520 | tf_op jit(solution)/shard_map/dot_general | solution.py:24
  640.0 15.1 %collective-permute-done.94 = bf16[256,1536]{1,0:T(8,128)(2,1)S(1)} collective-permute-done((bf16[256,1536]{1,0:T(8,128)(2,1)S(1)}, bf16[256,1536]{1,0:T(8,128)(2,1)S(1)}, u32[]{:S(2)}, u32[]{:S(2)}) %collective-permute-start.94) | collective-permute-done | bytes 786464 | tf_op jit(solution)/shard_map/ppermute | solution.py:260
  679.7 15.3 %collective-permute-done.96 = bf16[256,1536]{1,0:T(8,128)(2,1)} collective-permute-done((bf16[256,1536]{1,0:T(8,128)(2,1)}, bf16[256,1536]{1,0:T(8,128)(2,1)}, u32[]{:S(2)}, u32[]{:S(2)}) %collective-permute-start.96) | collective-permute-done | bytes 786464 | tf_op jit(solution)/shard_map/ppermute | solution.py:260
  697.8 13.9 %collective-permute-done.87 = bf16[256,1536]{1,0:T(8,128)(2,1)S(1)} collective-permute-done((bf16[256,1536]{1,0:T(8,128)(2,1)}, bf16[256,1536]{1,0:T(8,128)(2,1)S(1)}, u32[]{:S(2)}, u32[]{:S(2)}) %collective-permute-start.87) | collective-permute-done | bytes 786464 | tf_op jit(solution)/shard_map/ppermute | solution.py:260
  714.4 14.1 %collective-permute-done.105 = bf16[192,2048]{1,0:T(8,128)(2,1)S(1)} collective-permute-done((bf16[192,2048]{1,0:T(8,128)(2,1)S(1)}, bf16[192,2048]{1,0:T(8,128)(2,1)S(1)}, u32[]{:S(2)}, u32[]{:S(2)}) %collective-permute-start.105) | collective-permute-done | bytes 786464 | tf_op jit(solution)/shard_map/ppermute | solution.py:260
  731.0 14.4 %collective-permute-done.98 = bf16[256,1536]{1,0:T(8,128)(2,1)S(1)} collective-permute-done((bf16[256,1536]{1,0:T(8,128)(2,1)S(1)}, bf16[256,1536]{1,0:T(8,128)(2,1)S(1)}, u32[]{:S(2)}, u32[]{:S(2)}) %collective-permute-start.98) | collective-permute-done | bytes 786464 | tf_op jit(solution)/shard_map/ppermute | solution.py:260
  746.9 15.3 %collective-permute-done.89 = bf16[256,1536]{1,0:T(8,128)(2,1)S(1)} collective-permute-done((bf16[256,1536]{1,0:T(8,128)(2,1)S(1)}, bf16[256,1536]{1,0:T(8,128)(2,1)S(1)}, u32[]{:S(2)}, u32[]{:S(2)}) %collective-permute-start.89) | collective-permute-done | bytes 786464 | tf_op jit(solution)/shard_map/ppermute | solution.py:260
  781.0 13.0 %collective-permute-done.58 = bf16[512,2048]{1,0:T(8,128)(2,1)S(1)} collective-permute-done((bf16[512,2048]{1,0:T(8,128)(2,1)S(1)}, bf16[512,2048]{1,0:T(8,128)(2,1)S(1)}, u32[]{:S(2)}, u32[]{:S(2)}) %collective-permute-start.58) | collective-permute-done | bytes 2097184 | tf_op jit(solution)/shard_map/ppermute | solution.py:260
  796.0 43.0 %collective-permute-done.52 = bf16[512,2048]{1,0:T(8,128)(2,1)} collective-permute-done((bf16[512,2048]{1,0:T(8,128)(2,1)S(1)}, bf16[512,2048]{1,0:T(8,128)(2,1)}, u32[]{:S(2)}, u32[]{:S(2)}) %collective-permute-start.52) | collective-permute-done | bytes 2097184 | tf_op jit(solution)/shard_map/ppermute | solution.py:260
  860.9 39.9 %collective-permute-done.60 = bf16[512,2048]{1,0:T(8,128)(2,1)} collective-permute-done((bf16[512,2048]{1,0:T(8,128)(2,1)}, bf16[512,2048]{1,0:T(8,128)(2,1)}, u32[]{:S(2)}, u32[]{:S(2)}) %collective-permute-start.60) | collective-permute-done | bytes 2097184 | tf_op jit(solution)/shard_map/ppermute | solution.py:260
  903.8 13.9 %collective-permute-done.101 = bf16[128,2,1536]{2,0,1:T(8,128)(2,1)} collective-permute-done((bf16[128,2,1536]{2,0,1:T(8,128)(2,1)}, bf16[128,2,1536]{2,0,1:T(8,128)(2,1)}, u32[]{:S(2)}, u32[]{:S(2)}) %collective-permute-start.101) | collective-permute-done | bytes 786464 | tf_op jit(solution)/shard_map/ppermute | solution.py:260
  952.6 36.8 %attend_back.1 = (bf16[2048,1024]{1,0:T(8,128)(2,1)}, f32[8,128]{1,0:T(8,128)}, f32[8,128]{1,0:T(8,128)}) custom-call(s32[4]{0:T(128)} %select_n.715.nat_ref, f32[2048,1024]{1,0:T(8,128)} %fusion.26.lin_ref, bf16[2048,512]{1,0:T(8,128)(2,1)} %convolution_convert_fusion.7.do_ref, f32[2048,128]{1,0:T(8,128)} %get-tuple-element.143.cos_ref, ...), custom_call_target="tpu_custom_call" | custom-call | flops 7516192768 | bytes 16777216 | tf_op jit(solution)/shard_map/attend_back/pallas_call | solution.py:208
  1000.2 13.4 %convolution_convert_fusion.5 = bf16[2048,1024]{1,0:T(8,128)(2,1)S(1)} fusion(bf16[2048,1024]{1,0:T(8,128)(2,1)} %get-tuple-element.16, f32[2048]{0:T(1024)S(1)} %copy-done.40, f32[2048]{0:T(1024)S(1)} %copy-done.45, bf16[512,2048]{1,0:T(8,128)(2,1)} %collective-permute-done.2, bf16[512,2048]{1,0:T(8,128)(2,1)} %collective-permute-done.1, ...), kind=kOutput, calls=%fused_computation.59 | convolution fusion | flops 8638169088 | bytes 16793600 | tf_op jit(solution)/shard_map/dot_general | solution.py:24
  1019.0 15.7 %fusion.3 = (f32[2048]{0:T(1024)S(1)}, bf16[2048,2048]{1,0:T(8,128)(2,1)}) fusion(f32[2048]{0:T(1024)S(1)} %copy-done.45, bf16[512,2048]{1,0:T(8,128)(2,1)} %collective-permute-done.2, bf16[512,2048]{1,0:T(8,128)(2,1)} %collective-permute-done.1, bf16[512,2048]{1,0:T(8,128)(2,1)} %collective-permute-done, bf16[512,2048]{1,0:T(8,128)(2,1)S(1)} %bitcast.448, ...), kind=kOutput, calls=%fused_computation.6 | convolution fusion | flops 8640264192 | bytes 25182208 | tf_op jit(solution)/shard_map/dot_general | solution.py:24
  1078.4 43.5 %psum.7 = f32[4352]{0:T(1024)S(1)} all-reduce(f32[4352]{0:T(1024)S(1)} %pad_maximum_fusion.17), channel_id=1, replica_groups=mesh['dp'=4,'ctx'=2,'fsdp'=4] {'dp','ctx','fsdp'}, use_global_device_ids=true, to_apply=%region_7.8 | all-reduce | flops 4352 | bytes 34816 | tf_op jit(solution)/shard_map/psum | solution.py:497
  1155.7 34.8 %collective-permute-done.74 = bf16[128,2,1024]{2,0,1:T(8,128)(2,1)S(1)} collective-permute-done((bf16[128,2,1024]{2,0,1:T(8,128)(2,1)S(1)}, bf16[128,2,1024]{2,0,1:T(8,128)(2,1)S(1)}, u32[]{:S(2)}, u32[]{:S(2)}) %collective-permute-start.74) | collective-permute-done | bytes 524320 | tf_op jit(solution)/shard_map/ppermute | solution.py:260
  (515 shorter events, 554.1 us)
Async XLA Ops:
  0.7 156.3 %collective-permute-start = (bf16[512,2048]{1,0:T(8,128)(2,1)}, bf16[512,2048]{1,0:T(8,128)(2,1)}, u32[]{:S(2)}, u32[]{:S(2)}) collective-permute-start(bf16[512,2048]{1,0:T(8,128)(2,1)} %bitcast.443), channel_id=1, source_target_pairs={{0,4},{1,5},{2,6},{3,7},{4,0},{5,1},{6,2},{7,3},{8,12},{9,13},{10,... | collective-permute-start | bytes 6291464 | tf_op jit(solution)/shard_map/ppermute | solution.py:260
  3.7 185.0 %collective-permute-start.1 = (bf16[512,2048]{1,0:T(8,128)(2,1)}, bf16[512,2048]{1,0:T(8,128)(2,1)}, u32[]{:S(2)}, u32[]{:S(2)}) collective-permute-start(bf16[512,2048]{1,0:T(8,128)(2,1)} %bitcast.444), channel_id=1, source_target_pairs={{0,1},{1,0},{2,3},{3,2},{4,5},{5,4},{6,7},{7,6},{8,9},{9,8},{10,11... | collective-permute-start | bytes 6291464 | tf_op jit(solution)/shard_map/ppermute | solution.py:260
  12.3 57.1 %collective-permute-start.36 = (bf16[128,1536]{1,0:T(8,128)(2,1)S(1)}, bf16[128,1536]{1,0:T(8,128)(2,1)}, u32[]{:S(2)}, u32[]{:S(2)}) collective-permute-start(bf16[128,1536]{1,0:T(8,128)(2,1)S(1)} %bitcast.517), channel_id=1, source_target_pairs={{0,1},{1,0},{2,3},{3,2},{4,5},{5,4},{6,7},{7,6},{8,9},{9,8},{10,11... | collective-permute-start | bytes 1179656 | tf_op jit(solution)/shard_map/ppermute | solution.py:260
  57.2 60.2 %collective-permute-start.44 = (bf16[192,2048]{1,0:T(8,128)(2,1)S(1)}, bf16[192,2048]{1,0:T(8,128)(2,1)S(1)}, u32[]{:S(2)}, u32[]{:S(2)}) collective-permute-start(bf16[192,2048]{1,0:T(8,128)(2,1)S(1)} %copy-done.30), channel_id=1, source_target_pairs={{0,2},{1,3},{2,0},{3,1},{4,6},{5,7},{6,4},{7,5},{8,10},{9,11},{10,... | collective-permute-start | bytes 2359304 | tf_op jit(solution)/shard_map/ppermute | solution.py:260
  157.1 214.2 %collective-permute-start.54 = (bf16[512,2048]{1,0:T(8,128)(2,1)}, bf16[512,2048]{1,0:T(8,128)(2,1)}, u32[]{:S(2)}, u32[]{:S(2)}) collective-permute-start(bf16[512,2048]{1,0:T(8,128)(2,1)} %bitcast.82), channel_id=1, source_target_pairs={{0,4},{1,5},{2,6},{3,7},{4,0},{5,1},{6,2},{7,3},{8,12},{9,13},{10,... | collective-permute-start | bytes 6291464 | tf_op jit(solution)/shard_map/ppermute | solution.py:260
  170.1 69.7 %collective-permute-start.37 = (bf16[256,1536]{1,0:T(8,128)(2,1)S(1)}, bf16[256,1536]{1,0:T(8,128)(2,1)}, u32[]{:S(2)}, u32[]{:S(2)}) collective-permute-start(bf16[256,1536]{1,0:T(8,128)(2,1)S(1)} %pad_maximum_fusion.12), channel_id=1, source_target_pairs={{0,2},{1,3},{2,0},{3,1},{4,6},{5,7},{6,4},{7,5},{8,10},{9,11},{10,... | collective-permute-start | bytes 2359304 | tf_op jit(solution)/shard_map/ppermute | solution.py:260
  184.6 57.5 %collective-permute-start.38 = (bf16[256,1536]{1,0:T(8,128)(2,1)S(1)}, bf16[256,1536]{1,0:T(8,128)(2,1)}, u32[]{:S(2)}, u32[]{:S(2)}) collective-permute-start(bf16[256,1536]{1,0:T(8,128)(2,1)S(1)} %pad_maximum_fusion.12), channel_id=1, source_target_pairs={{0,8},{1,9},{2,10},{3,11},{4,12},{5,13},{6,14},{7,15},{8,16},{9,17... | collective-permute-start | bytes 2359304 | tf_op jit(solution)/shard_map/ppermute | solution.py:260
  188.7 56.7 %collective-permute-start.29 = (bf16[256,1536]{1,0:T(8,128)(2,1)}, bf16[256,1536]{1,0:T(8,128)(2,1)S(1)}, u32[]{:S(2)}, u32[]{:S(2)}) collective-permute-start(bf16[256,1536]{1,0:T(8,128)(2,1)} %pad_maximum_fusion.11), channel_id=1, source_target_pairs={{0,2},{1,3},{2,0},{3,1},{4,6},{5,7},{6,4},{7,5},{8,10},{9,11},{10,... | collective-permute-start | bytes 2359304 | tf_op jit(solution)/shard_map/ppermute | solution.py:260
  189.8 57.3 %collective-permute-start.30 = (bf16[256,1536]{1,0:T(8,128)(2,1)}, bf16[256,1536]{1,0:T(8,128)(2,1)S(1)}, u32[]{:S(2)}, u32[]{:S(2)}) collective-permute-start(bf16[256,1536]{1,0:T(8,128)(2,1)} %pad_maximum_fusion.11), channel_id=1, source_target_pairs={{0,8},{1,9},{2,10},{3,11},{4,12},{5,13},{6,14},{7,15},{8,16},{9,17... | collective-permute-start | bytes 2359304 | tf_op jit(solution)/shard_map/ppermute | solution.py:260
  371.3 78.2 %collective-permute-start.55 = (bf16[512,2048]{1,0:T(8,128)(2,1)}, bf16[512,2048]{1,0:T(8,128)(2,1)}, u32[]{:S(2)}, u32[]{:S(2)}) collective-permute-start(bf16[512,2048]{1,0:T(8,128)(2,1)} %bitcast.82), channel_id=1, source_target_pairs={{0,1},{1,0},{2,3},{3,2},{4,5},{5,4},{6,7},{7,6},{8,9},{9,8},{10,11... | collective-permute-start | bytes 6291464 | tf_op jit(solution)/shard_map/ppermute | solution.py:260
  385.9 63.5 %collective-permute-start.56 = (bf16[512,2048]{1,0:T(8,128)(2,1)}, bf16[512,2048]{1,0:T(8,128)(2,1)}, u32[]{:S(2)}, u32[]{:S(2)}) collective-permute-start(bf16[512,2048]{1,0:T(8,128)(2,1)} %collective-permute-done.54), channel_id=1, source_target_pairs={{0,1},{1,0},{2,3},{3,2},{4,5},{5,4},{6,7},{7,6},{8,9},{9,8},{10,11... | collective-permute-start | bytes 6291464 | tf_op jit(solution)/shard_map/ppermute | solution.py:260
  502.6 169.8 %collective-permute-start.51 = (bf16[512,2048]{1,0:T(8,128)(2,1)}, bf16[512,2048]{1,0:T(8,128)(2,1)}, u32[]{:S(2)}, u32[]{:S(2)}) collective-permute-start(bf16[512,2048]{1,0:T(8,128)(2,1)} %get-tuple-element.77), channel_id=1, source_target_pairs={{0,1},{1,0},{2,3},{3,2},{4,5},{5,4},{6,7},{7,6},{8,9},{9,8},{10,11... | collective-permute-start | bytes 6291464 | tf_op jit(solution)/shard_map/ppermute | solution.py:260
  542.1 71.8 %collective-permute-start.102 = (bf16[192,2048]{1,0:T(8,128)(2,1)}, bf16[192,2048]{1,0:T(8,128)(2,1)}, u32[]{:S(2)}, u32[]{:S(2)}) collective-permute-start(bf16[192,2048]{1,0:T(8,128)(2,1)} %get-tuple-element.81), channel_id=1, source_target_pairs={{0,2},{1,3},{2,0},{3,1},{4,6},{5,7},{6,4},{7,5},{8,10},{9,11},{10,... | collective-permute-start | bytes 2359304 | tf_op jit(solution)/shard_map/ppermute | solution.py:260
  544.2 88.8 %collective-permute-start.104 = (bf16[192,2048]{1,0:T(8,128)(2,1)}, bf16[192,2048]{1,0:T(8,128)(2,1)}, u32[]{:S(2)}, u32[]{:S(2)}) collective-permute-start(bf16[192,2048]{1,0:T(8,128)(2,1)} %get-tuple-element.84), channel_id=1, source_target_pairs={{0,2},{1,3},{2,0},{3,1},{4,6},{5,7},{6,4},{7,5},{8,10},{9,11},{10,... | collective-permute-start | bytes 2359304 | tf_op jit(solution)/shard_map/ppermute | solution.py:260
  566.9 49.6 %collective-permute-start.93 = (bf16[256,1536]{1,0:T(8,128)(2,1)}, bf16[256,1536]{1,0:T(8,128)(2,1)}, u32[]{:S(2)}, u32[]{:S(2)}) collective-permute-start(bf16[256,1536]{1,0:T(8,128)(2,1)} %get-tuple-element.85), channel_id=1, source_target_pairs={{0,2},{1,3},{2,0},{3,1},{4,6},{5,7},{6,4},{7,5},{8,10},{9,11},{10,... | collective-permute-start | bytes 2359304 | tf_op jit(solution)/shard_map/ppermute | solution.py:260
  567.8 65.3 %collective-permute-start.95 = (bf16[256,1536]{1,0:T(8,128)(2,1)}, bf16[256,1536]{1,0:T(8,128)(2,1)}, u32[]{:S(2)}, u32[]{:S(2)}) collective-permute-start(bf16[256,1536]{1,0:T(8,128)(2,1)} %get-tuple-element.88), channel_id=1, source_target_pairs={{0,2},{1,3},{2,0},{3,1},{4,6},{5,7},{6,4},{7,5},{8,10},{9,11},{10,... | collective-permute-start | bytes 2359304 | tf_op jit(solution)/shard_map/ppermute | solution.py:260
  655.1 124.6 %collective-permute-start.59 = (bf16[512,2048]{1,0:T(8,128)(2,1)}, bf16[512,2048]{1,0:T(8,128)(2,1)S(1)}, u32[]{:S(2)}, u32[]{:S(2)}) collective-permute-start(bf16[512,2048]{1,0:T(8,128)(2,1)} %get-tuple-element.76), channel_id=1, source_target_pairs={{0,1},{1,0},{2,3},{3,2},{4,5},{5,4},{6,7},{7,6},{8,9},{9,8},{10,11... | collective-permute-start | bytes 6291464 | tf_op jit(solution)/shard_map/ppermute | solution.py:260
  745.4 48.6 %collective-permute-start.58 = (bf16[512,2048]{1,0:T(8,128)(2,1)S(1)}, bf16[512,2048]{1,0:T(8,128)(2,1)S(1)}, u32[]{:S(2)}, u32[]{:S(2)}) collective-permute-start(bf16[512,2048]{1,0:T(8,128)(2,1)S(1)} %fusion.18), channel_id=1, source_target_pairs={{0,4},{1,5},{2,6},{3,7},{4,0},{5,1},{6,2},{7,3},{8,12},{9,13},{10,... | collective-permute-start | bytes 6291464 | tf_op jit(solution)/shard_map/ppermute | solution.py:260
  762.6 76.4 %collective-permute-start.52 = (bf16[512,2048]{1,0:T(8,128)(2,1)S(1)}, bf16[512,2048]{1,0:T(8,128)(2,1)}, u32[]{:S(2)}, u32[]{:S(2)}) collective-permute-start(bf16[512,2048]{1,0:T(8,128)(2,1)S(1)} %fusion.22), channel_id=1, source_target_pairs={{0,4},{1,5},{2,6},{3,7},{4,0},{5,1},{6,2},{7,3},{8,12},{9,13},{10,... | collective-permute-start | bytes 6291464 | tf_op jit(solution)/shard_map/ppermute | solution.py:260
  778.7 122.2 %collective-permute-start.109 = (bf16[192,2048]{1,0:T(8,128)(2,1)}, bf16[192,2048]{1,0:T(8,128)(2,1)}, u32[]{:S(2)}, u32[]{:S(2)}) collective-permute-start(bf16[192,2048]{1,0:T(8,128)(2,1)} %get-tuple-element.61), channel_id=1, source_target_pairs={{0,4},{1,5},{2,6},{3,7},{4,0},{5,1},{6,2},{7,3},{8,12},{9,13},{10,... | collective-permute-start | bytes 2359304 | tf_op jit(solution)/shard_map/ppermute | solution.py:260
  780.4 71.0 %collective-permute-start.91 = (bf16[128,1536]{1,0:T(8,128)(2,1)}, bf16[128,1536]{1,0:T(8,128)(2,1)}, u32[]{:S(2)}, u32[]{:S(2)}) collective-permute-start(bf16[128,1536]{1,0:T(8,128)(2,1)} %dynamic-slice_bitcast_fusion.17), channel_id=1, source_target_pairs={{0,1},{1,0},{2,3},{3,2},{4,5},{5,4},{6,7},{7,6},{8,9},{9,8},{10,11... | collective-permute-start | bytes 1179656 | tf_op jit(solution)/shard_map/ppermute | solution.py:260
  846.7 54.1 %collective-permute-start.60 = (bf16[512,2048]{1,0:T(8,128)(2,1)}, bf16[512,2048]{1,0:T(8,128)(2,1)}, u32[]{:S(2)}, u32[]{:S(2)}) collective-permute-start(bf16[512,2048]{1,0:T(8,128)(2,1)} %get-tuple-element.62), channel_id=1, source_target_pairs={{0,4},{1,5},{2,6},{3,7},{4,0},{5,1},{6,2},{7,3},{8,12},{9,13},{10,... | collective-permute-start | bytes 6291464 | tf_op jit(solution)/shard_map/ppermute | solution.py:260
  847.7 70.0 %collective-permute-start.101 = (bf16[128,2,1536]{2,0,1:T(8,128)(2,1)}, bf16[128,2,1536]{2,0,1:T(8,128)(2,1)}, u32[]{:S(2)}, u32[]{:S(2)}) collective-permute-start(bf16[128,2,1536]{2,0,1:T(8,128)(2,1)} %pad_maximum_fusion.14), channel_id=1, source_target_pairs={{0,4},{1,5},{2,6},{3,7},{4,0},{5,1},{6,2},{7,3},{8,12},{9,13},{10,... | collective-permute-start | bytes 2359304 | tf_op jit(solution)/shard_map/ppermute | solution.py:260
  852.7 78.0 %collective-permute-start.92 = (bf16[128,2,1536]{2,0,1:T(8,128)(2,1)S(1)}, bf16[128,2,1536]{2,0,1:T(8,128)(2,1)}, u32[]{:S(2)}, u32[]{:S(2)}) collective-permute-start(bf16[128,2,1536]{2,0,1:T(8,128)(2,1)S(1)} %pad_maximum_fusion.13), channel_id=1, source_target_pairs={{0,4},{1,5},{2,6},{3,7},{4,0},{5,1},{6,2},{7,3},{8,12},{9,13},{10,... | collective-permute-start | bytes 2359304 | tf_op jit(solution)/shard_map/ppermute | solution.py:260
  860.9 83.0 %collective-permute-start.61 = (bf16[512,2048]{1,0:T(8,128)(2,1)}, bf16[512,2048]{1,0:T(8,128)(2,1)}, u32[]{:S(2)}, u32[]{:S(2)}) collective-permute-start(bf16[512,2048]{1,0:T(8,128)(2,1)} %get-tuple-element.62), channel_id=1, source_target_pairs={{0,1},{1,0},{2,3},{3,2},{4,5},{5,4},{6,7},{7,6},{8,9},{9,8},{10,11... | collective-permute-start | bytes 6291464 | tf_op jit(solution)/shard_map/ppermute | solution.py:260
  999.4 48.6 %collective-permute-start.79 = (bf16[64,2048]{1,0:T(8,128)(2,1)}, bf16[64,2048]{1,0:T(8,128)(2,1)S(1)}, u32[]{:S(2)}, u32[]{:S(2)}) collective-permute-start(bf16[64,2048]{1,0:T(8,128)(2,1)} %get-tuple-element.100), channel_id=1, source_target_pairs={{0,2},{1,3},{2,0},{3,1},{4,6},{5,7},{6,4},{7,5},{8,10},{9,11},{10,... | collective-permute-start | bytes 786440 | tf_op jit(solution)/shard_map/ppermute | solution.py:260
  1041.5 85.5 %collective-permute-start.63 = (bf16[512,2048]{1,0:T(8,128)(2,1)}, bf16[512,2048]{1,0:T(8,128)(2,1)}, u32[]{:S(2)}, u32[]{:S(2)}) collective-permute-start(bf16[512,2048]{1,0:T(8,128)(2,1)} %get-tuple-element.73), channel_id=1, source_target_pairs={{0,1},{1,0},{2,3},{3,2},{4,5},{5,4},{6,7},{7,6},{8,9},{9,8},{10,11... | collective-permute-start | bytes 6291464 | tf_op jit(solution)/shard_map/ppermute | solution.py:260
  1057.0 66.0 %collective-permute-start.70 = (bf16[256,1024]{1,0:T(8,128)(2,1)}, bf16[256,1024]{1,0:T(8,128)(2,1)}, u32[]{:S(2)}, u32[]{:S(2)}) collective-permute-start(bf16[256,1024]{1,0:T(8,128)(2,1)} %get-tuple-element.95), channel_id=1, source_target_pairs={{0,2},{1,3},{2,0},{3,1},{4,6},{5,7},{6,4},{7,5},{8,10},{9,11},{10,... | collective-permute-start | bytes 1572872 | tf_op jit(solution)/shard_map/ppermute | solution.py:260
  1059.3 72.2 %collective-permute-start.72 = (bf16[256,1024]{1,0:T(8,128)(2,1)}, bf16[256,1024]{1,0:T(8,128)(2,1)S(1)}, u32[]{:S(2)}, u32[]{:S(2)}) collective-permute-start(bf16[256,1024]{1,0:T(8,128)(2,1)} %get-tuple-element.94), channel_id=1, source_target_pairs={{0,2},{1,3},{2,0},{3,1},{4,6},{5,7},{6,4},{7,5},{8,10},{9,11},{10,... | collective-permute-start | bytes 1572872 | tf_op jit(solution)/shard_map/ppermute | solution.py:260
  1066.8 58.6 %collective-permute-start.69 = (bf16[256,1024]{1,0:T(8,128)(2,1)}, bf16[256,1024]{1,0:T(8,128)(2,1)S(1)}, u32[]{:S(2)}, u32[]{:S(2)}) collective-permute-start(bf16[256,1024]{1,0:T(8,128)(2,1)} %fusion.57), channel_id=1, source_target_pairs={{0,8},{1,9},{2,10},{3,11},{4,12},{5,13},{6,14},{7,15},{8,16},{9,17... | collective-permute-start | bytes 1572872 | tf_op jit(solution)/shard_map/ppermute | solution.py:260
  1123.0 81.5 %collective-permute-start.65 = (bf16[512,2048]{1,0:T(8,128)(2,1)}, bf16[512,2048]{1,0:T(8,128)(2,1)}, u32[]{:S(2)}, u32[]{:S(2)}) collective-permute-start(bf16[512,2048]{1,0:T(8,128)(2,1)} %get-tuple-element.74), channel_id=1, source_target_pairs={{0,1},{1,0},{2,3},{3,2},{4,5},{5,4},{6,7},{7,6},{8,9},{9,8},{10,11... | collective-permute-start | bytes 6291464 | tf_op jit(solution)/shard_map/ppermute | solution.py:260
  1131.4 73.2 %collective-permute-start.64 = (bf16[512,2048]{1,0:T(8,128)(2,1)}, bf16[512,2048]{1,0:T(8,128)(2,1)}, u32[]{:S(2)}, u32[]{:S(2)}) collective-permute-start(bf16[512,2048]{1,0:T(8,128)(2,1)} %fusion.16), channel_id=1, source_target_pairs={{0,4},{1,5},{2,6},{3,7},{4,0},{5,1},{6,2},{7,3},{8,12},{9,13},{10,... | collective-permute-start | bytes 6291464 | tf_op jit(solution)/shard_map/ppermute | solution.py:260
  (140 other events, 3098.0 us)

commit v2 on v1

--- a/solution.py
+++ b/solution.py
@@ -239,6 +239,479 @@
     )(nat, lin, d_out, cosine, sine, gq, gk)
 
 
+ANY = pl.BlockSpec(memory_space=pl.ANY)
+IN_VMEM = pl.BlockSpec(memory_space=pltpu.VMEM)
+SEMAPHORES = 128
+
+
+class Flight:
+    def __init__(self, made, remote):
+        self.made, self.remote, self.started, self.left = made, remote, False, True
+
+    def start(self):
+        self.made.start()
+
+    def wait(self):
+        if self.left:
+            self.left = False
+            if self.remote:
+                self.made.wait_recv()
+            else:
+                self.made.wait()
+
+    wait_recv = wait
+
+
+class Mover:
+    def __init__(self, grid, local_sems, send_sems, recv_sems):
+        self.grid = grid
+        self.z, self.y, self.a, self.c = grid.index()
+        self.local_sems, self.send_sems, self.recv_sems = local_sems, send_sems, recv_sems
+        self.locals, self.remotes, self.made_count = [], [], 0
+
+    def device(self, z, y, a, c):
+        return {"dp": z, "ctx": y, "fsdp": a * self.grid.C + c}
+
+    def peer(self, z=0, y=0, a=0, c=0):
+        g = self.grid
+        return self.device(
+            lax.rem(self.z + z + g.Z, g.Z), lax.rem(self.y + y + g.Y, g.Y),
+            lax.rem(self.a + a + g.A, g.A), lax.rem(self.c + c + g.C, g.C),
+        )
+
+    def meet(self, extra=()):
+        g = self.grid
+        offsets = set()
+        for axis, size in enumerate(g.shape):
+            for step in (1, size - 1):
+                if 0 < step < size:
+                    offsets.add(tuple(step if i == axis else 0 for i in range(4)))
+        barrier = pltpu.get_barrier_semaphore()
+        for offset in sorted(offsets):
+            pl.semaphore_signal(
+                barrier, inc=1, device_id=self.peer(*offset), device_id_type=pl.DeviceIdType.MESH
+            )
+        for device, present in extra:
+
+            @pl.when(present)
+            def _(device=device):
+                pl.semaphore_signal(
+                    barrier, inc=1, device_id=device, device_id_type=pl.DeviceIdType.MESH
+                )
+
+        count = len(offsets)
+        for _, present in extra:
+            count = count + present.astype(jnp.int32)
+        pl.semaphore_wait(barrier, count)
+
+    def copy(self, src, dst):
+        made = Flight(pltpu.make_async_copy(src, dst, self.local_sems.at[len(self.locals)]), False)
+        self.locals.append(made)
+        made.start()
+        return made
+
+    def make(self, src, dst, device):
+        i = self.made_count
+        made = pltpu.make_async_remote_copy(
+            src_ref=src, dst_ref=dst, send_sem=self.send_sems.at[i], recv_sem=self.recv_sems.at[i],
+            device_id=device, device_id_type=pl.DeviceIdType.MESH,
+        )
+        self.made_count = i + 1
+        return made
+
+    def send(self, src, dst, **to):
+        made = Flight(self.make(src, dst, self.peer(**to)), True)
+        self.remotes.append(made)
+        made.start()
+        return made
+
+    def settle(self):
+        for made in self.remotes:
+            made.wait()
+        for made in self.locals:
+            made.wait()
+        for made in self.remotes:
+            made.made.wait_send()
+
+
+def semaphores():
+    return [pltpu.SemaphoreType.DMA((SEMAPHORES,)) for _ in range(3)]
+
+
+class Ring:
+    def __init__(self, mover, full):
+        self.m, self.full = mover, full
+        self.hops, self.sides = {}, {}
+
+    def block(self, s, k=0):
+        g = self.m.grid
+        return self.full.at[
+            lax.rem(self.m.z - s + g.Z, g.Z), lax.rem(self.m.a - k + g.A, g.A)
+        ]
+
+    def hop(self, s):
+        src = self.block(s - 1)
+        self.hops[s] = self.m.send(src, src, z=1)
+
+    def landed(self, s):
+        self.hops[s].wait_recv()
+
+    def side(self, s):
+        src = self.block(s)
+        self.sides[s] = [self.m.send(src, src, a=1)]
+
+    def finish_side(self, s):
+        for k in range(1, self.m.grid.A):
+            self.sides[s][k - 1].wait_recv()
+            if k < self.m.grid.A - 1:
+                src = self.block(s, k)
+                self.sides[s].append(self.m.send(src, src, a=1))
+
+
+def gather_start_kernel(
+    grid, out_target, out_source, tok, pos, pack, qkv_pair, out_own, gate_pair, up_pair, down_own,
+    tok_all, pos_all, qkv_full, out_full, gate_full, up_full, down_full,
+    local_sems, send_sems, recv_sems,
+):
+    m = Mover(grid, local_sems, send_sems, recv_sems)
+    Z, Y, A, C = grid.shape
+    target, source = out_target(m.z, m.y, m.a, m.c), out_source(m.z, m.y, m.a, m.c)
+    away = (target[0] != m.z) | (target[1] != m.y) | (target[2] != m.a) | (target[3] != m.c)
+    m.meet([(m.device(*target), away), (m.device(*source), away)])
+
+    class Tokens:
+        def __init__(self, own, whole):
+            self.own, self.whole, self.flights, self.cores = own, whole, {}, []
+
+        def step(self, k):
+            src = self.own if k == 1 else self.whole.at[0, Y - k + 1]
+            self.flights[k] = m.send(src, self.whole.at[0, Y - k], y=1)
+
+        def keep(self):
+            if C == 2:
+                m.send(self.own, self.whole.at[1, 0], c=1)
+            m.copy(self.own, self.whole.at[0, 0])
+
+        def landed(self, k):
+            self.flights[k].wait_recv()
+            if k < Y - 1:
+                self.step(k + 1)
+            if C == 2:
+                m.send(self.whole.at[0, Y - k], self.whole.at[1, Y - k], c=1)
+
+    toks, poss = Tokens(tok, tok_all), Tokens(pos, pos_all)
+
+    class Pair:
+        def __init__(self, own, other, mine, yours):
+            self.local = m.copy(own, mine)
+            self.other = m.send(other, yours, c=1) if C == 2 else None
+
+        def wait(self):
+            self.local.wait()
+            if C == 2:
+                self.other.wait_recv()
+
+    def columns(shard, full):
+        at = full.at[m.z, m.a, m.c]
+        return Pair(shard.at[m.c], shard.at[(C - 1) * (1 - m.c)], at, at)
+
+    rows = out_own.shape[0] // Y
+    mine = out_own.at[pl.ds(pl.multiple_of(m.y * rows, rows), rows)]
+    moved = m.make(mine, out_full.at[target[0], target[2], pl.ds(0, rows)], m.device(*target))
+    stay = pltpu.make_async_copy(
+        mine, out_full.at[m.z, m.a, pl.ds(0, rows)], m.local_sems.at[SEMAPHORES - 1]
+    )
+
+    @pl.when(away)
+    def _():
+        moved.start()
+
+    @pl.when(jnp.logical_not(away))
+    def _():
+        stay.start()
+
+    qkv_pairs = columns(qkv_pair, qkv_full)
+    if Y > 1:
+        poss.step(1)
+        toks.step(1)
+    at = out_full.at[m.z, m.a, pl.ds(pl.multiple_of(rows + m.c * 8, 8), 8)]
+    packs = Pair(pack, pack, at, at)
+    gate_pairs = columns(gate_pair, gate_full)
+    qkv, out, gate = Ring(m, qkv_full), Ring(m, out_full), Ring(m, gate_full)
+    qkv_pairs.wait()
+    if Z > 1:
+        qkv.hop(1)
+    qkv.side(0)
+    up_pairs = columns(up_pair, up_full)
+    rows = down_own.shape[0] // Y
+    m.copy(down_own.at[pl.ds(pl.multiple_of(m.y * rows, rows), rows)], down_full.at[m.z, m.a])
+    for part in (toks, poss):
+        part.keep()
+    for k in range(1, Y):
+        poss.landed(k)
+    for s in range(1, Z):
+        if s == Z - 1:
+            for k in range(1, Y):
+                toks.landed(k)
+        qkv.landed(s)
+        if s < Z - 1:
+            qkv.hop(s + 1)
+        qkv.side(s)
+        if s == Z - 2:
+            gate_pairs.wait()
+            gate.hop(1)
+    packs.wait()
+
+    @pl.when(away)
+    def _():
+        moved.wait_recv()
+
+    @pl.when(jnp.logical_not(away))
+    def _():
+        stay.wait()
+
+    if Z > 1:
+        out.hop(1)
+    out.side(0)
+    gate.side(0)
+    if Z > 2:
+        gate.landed(1)
+        gate.hop(2)
+    for s in range(1, Z):
+        out.landed(s)
+        if s < Z - 1:
+            out.hop(s + 1)
+        out.side(s)
+    for ring in (qkv, out):
+        for s in range(Z):
+            ring.finish_side(s)
+    gate.finish_side(0)
+    m.settle()
+
+    @pl.when(away)
+    def _():
+        moved.wait_send()
+
+
+def weights_program(gate, up, down, Z):
+    def first():
+        if Z > 3:
+            gate.hop(3)
+        up.hop(1)
+        for s in range(1, min(Z, 3)):
+            gate.side(s)
+
+    yield first
+    for s in range(3, Z):
+
+        def more(s=s):
+            gate.landed(s)
+            if s < Z - 1:
+                gate.hop(s + 1)
+            gate.side(s)
+
+        yield more
+    for s in range(1, Z):
+
+        def rest(s=s):
+            up.landed(s)
+            if s < Z - 1:
+                up.hop(s + 1)
+            else:
+                down.hop(1)
+            if s == 1:
+                up.side(0)
+            up.side(s)
+
+        yield rest
+    for s in range(1, Z):
+
+        def tail(s=s):
+            down.landed(s)
+            if s < Z - 1:
+                down.hop(s + 1)
+
+        yield tail
+
+    def finish():
+        for s in range(1, Z):
+            gate.finish_side(s)
+        for s in range(Z):
+            up.finish_side(s)
+
+    yield finish
+
+
+def join_kernel(
+    grid, halves, background, part, own, gain, gate_in, up_in, down_in,
+    mid, h2, gate_full, up_full, down_full,
+    mine, other, passing, landing, base, total, low, local_sems, send_sems, recv_sems,
+):
+    m = Mover(grid, local_sems, send_sems, recv_sems)
+    Z, Y, A, C = grid.shape
+    m.meet()
+    rows = own.shape[0]
+    n = rows // halves
+    loads = {}
+    crossings = {}
+    for h in range(halves):
+        for j in reversed(range(Y)):
+            at = pl.ds(h * n, n)
+            if C == 2:
+                crossings[h, j] = m.send(part.at[1, j, at], other.at[j, at], c=1)
+            loads[h, j] = m.copy(part.at[0, j, at], mine.at[j, at])
+    own_load = m.copy(own, base)
+    gate, up, down = Ring(m, gate_full), Ring(m, up_full), Ring(m, down_full)
+    program = list(background(gate, up, down, Z))
+
+    def run(count):
+        for _ in range(min(count, len(program))):
+            program.pop(0)()
+
+    chunk = min(32, n)
+
+    def each(h, body):
+        @pl.loop(0, n // chunk)
+        def _(i):
+            body(pl.ds(pl.multiple_of(h * n + i * chunk, chunk), chunk))
+
+    def summed(j, at):
+        value = mine[j, at].astype(F32)
+        return value + other[j, at].astype(F32) if C == 2 else value
+
+    def ready(h, j):
+        loads[h, j].wait()
+        if C == 2:
+            crossings[h, j].wait_recv()
+
+    run(1)
+    flights = {}
+    for h in range(halves):
+        ready(h, Y - 1)
+
+        def first(at):
+            passing[0, at] = summed(Y - 1, at).astype(BF)
+
+        each(h, first)
+        if Y > 1:
+            at = pl.ds(h * n, n)
+            flights[h, 1] = m.send(passing.at[0, at], landing.at[0, at], y=1)
+    for k in range(2, Y):
+        for h in range(halves):
+            flights[h, k - 1].wait_recv()
+            ready(h, Y - k)
+
+            def middle(at, k=k):
+                value = landing[k - 2, at].astype(F32) + summed(Y - k, at)
+                passing[k - 1, at] = value.astype(BF)
+
+            each(h, middle)
+            at = pl.ds(h * n, n)
+            flights[h, k] = m.send(passing.at[k - 1, at], landing.at[k - 1, at], y=1)
+    own_load.wait()
+    run(2)
+    stores, spread = [], {}
+    for h in range(halves):
+        if Y > 1:
+            ready(h, 0)
+            flights[h, Y - 1].wait_recv()
+
+        def last(at):
+            value = base[at].astype(F32) + (
+                summed(0, at) + landing[Y - 2, at].astype(F32) if Y > 1 else passing[0, at].astype(F32)
+            )
+            total[at] = value
+            scale = lax.rsqrt(jnp.mean(value * value, axis=-1, keepdims=True) + EPS)
+            low[at] = (value * scale * gain[...]).astype(BF)
+
+        each(h, last)
+        at = pl.ds(h * n, n)
+        if Y > 1:
+            spread[h, 1] = m.send(low.at[at], h2.at[0, Y - 1, at], y=1)
+        if C == 2:
+            spread[h, "core"] = m.send(low.at[at], h2.at[1, 0, at], c=1)
+        stores.append(m.copy(low.at[at], h2.at[0, 0, at]))
+        stores.append(m.copy(total.at[at], mid.at[at]))
+        run(1)
+    run(2)
+    for k in range(1, Y):
+        for h in range(halves):
+            at = pl.ds(h * n, n)
+            spread[h, k].wait_recv()
+            if k < Y - 1:
+                spread[h, k + 1] = m.send(h2.at[0, Y - k, at], h2.at[0, Y - k - 1, at], y=1)
+            if C == 2:
+                spread[h, "core", k] = m.send(h2.at[0, Y - k, at], h2.at[1, Y - k, at], c=1)
+    run(len(program))
+    m.settle()
+
+
+def gather_start(grid, targets, tok, pos, pack, qkv_pair, out_own, gate_pair, up_pair, down_own):
+    Z, Y, A, C = grid.shape
+
+    def whole(own, *lead):
+        return jax.ShapeDtypeStruct(lead + own.shape, own.dtype)
+
+    def cut(own):
+        return jax.ShapeDtypeStruct((Z, A, own.shape[0] // Y) + own.shape[1:], own.dtype)
+
+    shapes = [whole(tok, C, Y), whole(pos, C, Y), whole(qkv_pair, Z, A)]
+    out_rows = out_own.shape[0] // Y + 8 * C
+    shapes += [jax.ShapeDtypeStruct((Z, A, out_rows, out_own.shape[1]), BF), whole(gate_pair, Z, A), whole(up_pair, Z, A), cut(down_own)]
+    return pl.pallas_call(
+        functools.partial(gather_start_kernel, grid, *targets),
+        out_shape=shapes,
+        in_specs=[IN_VMEM] * 8,
+        out_specs=[ANY] * 7,
+        scratch_shapes=semaphores(),
+        compiler_params=pltpu.CompilerParams(
+            collective_id=0, has_side_effects=True, vmem_limit_bytes=32 * 1024 * 1024
+        ),
+        cost_estimate=pl.CostEstimate(flops=0, bytes_accessed=300_000_000, transcendentals=0),
+        name="gather_start",
+    )(tok, pos, pack, qkv_pair, out_own, gate_pair, up_pair, down_own)
+
+
+def join(grid, part, own, gain, gate, up, down):
+    Z, Y, A, C = grid.shape
+    rows, width = own.shape
+    halves = 2 if rows % 64 == 0 else 1
+    hops = max(Y - 1, 1)
+    return pl.pallas_call(
+        functools.partial(join_kernel, grid, halves, weights_program),
+        out_shape=[
+            jax.ShapeDtypeStruct((rows, width), F32),
+            jax.ShapeDtypeStruct((C, Y, rows, width), BF),
+            jax.ShapeDtypeStruct(gate.shape, gate.dtype),
+            jax.ShapeDtypeStruct(up.shape, up.dtype),
+            jax.ShapeDtypeStruct(down.shape, down.dtype),
+        ],
+        in_specs=[ANY, ANY, IN_VMEM, ANY, ANY, ANY],
+        out_specs=[ANY] * 5,
+        input_output_aliases={3: 2, 4: 3, 5: 4},
+        scratch_shapes=[
+            pltpu.VMEM((Y, rows, width), BF),
+            pltpu.VMEM((Y, rows, width), BF),
+            pltpu.VMEM((hops, rows, width), BF),
+            pltpu.VMEM((hops, rows, width), BF),
+            pltpu.VMEM((rows, width), BF),
+            pltpu.VMEM((rows, width), F32),
+            pltpu.VMEM((rows, width), BF),
+            *semaphores(),
+        ],
+        compiler_params=pltpu.CompilerParams(
+            collective_id=1, has_side_effects=True, vmem_limit_bytes=40 * 1024 * 1024
+        ),
+        cost_estimate=pl.CostEstimate(flops=0, bytes_accessed=300_000_000, transcendentals=0),
+        name="join",
+    )(part.reshape(C, Y, rows, width), own, gain, gate, up, down)
+
+
+def after(tokens, *values):
+    out = lax.optimization_barrier((*values, *tokens))
+    return out[0] if len(values) == 1 else out[: len(values)]
+
+
 class Grid:
     def __init__(self, mesh):
         self.Z, self.Y, self.F = (mesh.shape[n] for n in AXES)
@@ -303,44 +776,6 @@
         for k in range(1, Y):
             total = send(total.astype(BF), y=1).astype(F32) + summed[Y - 1 - k]
         return total
-
-    def gather_blocks(own):
-        buffer = jnp.zeros((Z, A) + own.shape, own.dtype)
-        held = own
-        for s in range(Z):
-            if s:
-                held = send(held, z=1)
-            piece = held
-            for k in range(A):
-                if k:
-                    piece = send(piece, a=1)
-                buffer = lax.dynamic_update_slice(
-                    buffer, piece[None, None], ((z - s) % Z, (a - k) % A) + (0,) * own.ndim
-                )
-        return buffer
-
-    def scatter_blocks(partial):
-        def term(i, j):
-            at = ((z + i) % Z, (a + j) % A) + (0,) * (partial.ndim - 2)
-            return lax.dynamic_slice(partial, at, (1, 1) + partial.shape[2:])[0, 0].astype(F32)
-
-        def over_a(i):
-            total = term(i, A - 1)
-            for k in range(1, A):
-                total = send(total.astype(BF), a=1).astype(F32) + term(i, A - 1 - k)
-            return total
-
-        total = over_a(Z - 1)
-        for s in range(1, Z):
-            total = send(total.astype(BF), z=1).astype(F32) + over_a(Z - 1 - s)
-        return total
-
-    def own_columns(shard):
-        own = lax.dynamic_slice_in_dim(shard, y * C + c, 1, 1)[:, 0]
-        if C == 1:
-            return own
-        other = send(lax.dynamic_slice_in_dim(shard, y * C + (1 - c), 1, 1)[:, 0], c=1)
-        return jnp.concatenate([jnp.where(c == 0, own, other), jnp.where(c == 0, other, own)], axis=0)
 
     def shard_of_columns(total):
         total = total.astype(BF)
@@ -362,9 +797,10 @@
         return whole
 
     shard_rows = w_query.shape[0]
+    n, m = gain_attn.shape[0], gain_query.shape[0]
     pack = jnp.concatenate([gain_attn, gain_mlp, gain_query, gain_key])
+    pack = jnp.pad(pack, (0, 8 * width - pack.shape[0])).reshape(8, width)
     qkv_width = (GROUP + 2) * HEAD_DIM * KV_HEADS // T
-    pack = jnp.pad(pack, (0, qkv_width * 8 - pack.shape[0])).reshape(8, 1, qkv_width)
     qkv_shard = jnp.concatenate(
         [
             w_query.reshape(shard_rows, KV_HEADS, GROUP * HEAD_DIM),
@@ -373,43 +809,41 @@
         ],
         axis=2,
     ).reshape(shard_rows, T, qkv_width)
-    qkv_shard = jnp.concatenate([qkv_shard, jnp.broadcast_to(pack, (8, T, qkv_width))], axis=0)
-
-    x_group = gather_tokens(tokens.reshape(rows, width))
-    place = gather_tokens(positions.reshape(rows, 1))[:, 0]
-
-    qkv_all = gather_blocks(own_columns(qkv_shard)).reshape(ZA * C, shard_rows + 8, qkv_width)
-    w_qkv = qkv_all[:, :shard_rows].reshape(width, qkv_width)
-    packs = qkv_all[:, shard_rows:].reshape(ZA * C, -1)
-    n, m = gain_attn.shape[0], gain_query.shape[0]
+
+    def out_target(i, j, k, l):
+        b = ((i * A + k) * C + l) * Y + j
+        rank, at = b // ZA, b % ZA
+        return (at // A, rank // C, at % A, rank % C)
+
+    def out_source(i, j, k, l):
+        b = (j * C + l) * ZA + i * A + k
+        shard, copy = b // Y, b % Y
+        return (shard // C // A, copy, shard // C % A, shard % C)
+
+    down_rows = w_down.shape[0] // Y
+
+    def hidden_columns(shard):
+        split = shard.reshape(shard.shape[0], ZA, C, Y, down_rows)
+        return split.transpose(0, 3, 2, 1, 4).reshape(shard.shape[0], T, ZA * down_rows)
+
+    def own_pair(shard):
+        return lax.dynamic_slice_in_dim(shard, y * C, C, 1).transpose(1, 0, 2)
+
+    lanes = 128 if rows % 128 == 0 else rows
+    tok_all, pos_all, w_qkv, w_out, gate_all, up_all, down_all = gather_start(
+        grid, (out_target, out_source), tokens.reshape(rows, width),
+        positions.reshape(rows // lanes, lanes), pack, own_pair(qkv_shard), w_output,
+        own_pair(hidden_columns(w_gate)), own_pair(hidden_columns(w_up)), w_down,
+    )
+    x_group = tok_all.reshape(group_tokens, width)
+    place = pos_all.reshape(group_tokens)
+    packs = w_out[:, :, -8 * C :].reshape(ZA * C, 8 * width)
     ga = packs[:, :n].reshape(1, width).astype(F32)
     gm = packs[:, n : 2 * n].reshape(1, width).astype(F32)
     gq = packs[:, 2 * n : 2 * n + m].reshape(1, HEAD_DIM).astype(F32)
     gk = packs[:, 2 * n + m : 2 * n + 2 * m].reshape(1, HEAD_DIM).astype(F32)
-
-    def out_target(i, j, k, l):
-        b = ((i * A + k) * C + l) * Y + j
-        rank, at = b // ZA, b % ZA
-        return (at // A, rank // C, at % A, rank % C)
-
-    def out_source(i, j, k, l):
-        b = (j * C + l) * ZA + i * A + k
-        shard, copy = b // Y, b % Y
-        return (shard // C // A, copy, shard // C % A, shard % C)
-
-    out_rows = w_output.shape[0] // Y
-    wo_block = grid.permute(lax.dynamic_slice_in_dim(w_output, y * out_rows, out_rows, 0), out_target)
-    w_out = gather_blocks(wo_block).reshape(-1, width)
-
-    down_rows = w_down.shape[0] // Y
-
-    def hidden_columns(shard):
-        split = shard.reshape(shard.shape[0], ZA, C, Y, down_rows)
-        return split.transpose(0, 3, 2, 1, 4).reshape(shard.shape[0], T, ZA * down_rows)
-
-    w_g = gather_blocks(own_columns(hidden_columns(w_gate))).reshape(width, -1)
-    w_u = gather_blocks(own_columns(hidden_columns(w_up))).reshape(width, -1)
-    w_d = gather_blocks(lax.dynamic_slice_in_dim(w_down, y * down_rows, down_rows, 0)).reshape(-1, width)
+    w_qkv = w_qkv.reshape(width, qkv_width)
+    w_out = w_out[:, :, : -8 * C].reshape(-1, width)
 
     freqs = THETA ** (-(jnp.arange(HALF, dtype=F32) * 2.0 / HEAD_DIM))
     angles = place.astype(F32)[:, None] * freqs
@@ -432,11 +866,19 @@
     lin = dot(h1, w_qkv)
     attended = attend(lin, cosine, sine, gq, gk, nat, seqs, heads, block)
     x_own = tokens.reshape(rows, width).astype(F32)
-    x_mid = x_own + scatter_tokens(dot(attended, w_out).astype(BF))
+    x_mid, h2, gate_all, up_all, down_all = join(
+        grid, dot(attended, w_out).astype(BF), tokens.reshape(rows, width), gm, gate_all, up_all, down_all
+    )
+    h2 = h2.reshape(group_tokens, width)
+    w_g, w_u = gate_all.reshape(width, -1), up_all.reshape(width, -1)
+    side = lax.dynamic_index_in_dim(down_all, a, 1, keepdims=False)
+    for k in range(1, A):
+        side = send(side, a=1)
+        down_all = lax.dynamic_update_slice(down_all, side[:, None], (0, (a - k) % A, 0, 0))
+    w_d = down_all.reshape(-1, width)
 
     mid_unit, mid_scale = unit_rows(x_mid)
-    h2 = gather_tokens((mid_unit * gm).astype(BF))
-    dy = gather_tokens(cotangent.reshape(rows, width))
+    dy = gather_tokens(after((h2,), cotangent.reshape(rows, width)))
     gate = dot(h2, w_g)
     upper = dot(h2, w_u)
     sigmoid = 1.0 / (1.0 + jnp.exp(-gate))
@@ -445,34 +887,12 @@
     gate_factor = (upper * sigmoid * (1.0 + gate * (1.0 - sigmoid))).astype(BF)
     upper_factor = silu.astype(BF)
     grad_down = dot(hidden, dy, TN).astype(BF)
-    output = x_mid + scatter_tokens(dot(hidden, w_d).astype(BF))
-    d_hidden = dot(dy, w_d, NT)
-    d_gate = (d_hidden * gate_factor.astype(F32)).astype(BF)
-    d_upper = (d_hidden * upper_factor.astype(F32)).astype(BF)
-    d_h2 = scatter_tokens((dot(d_gate, w_g, NT) + dot(d_upper, w_u, NT)).astype(BF))
-    grad_gate = dot(h2, d_gate, TN).astype(BF)
-    grad_up = dot(h2, d_upper, TN).astype(BF)
-    sum_mlp = jnp.sum(d_h2 * mid_unit, axis=0)
-    d_mid = cotangent.reshape(rows, width).astype(F32) + norm_back(d_h2, gm, mid_unit, mid_scale)
-
-    d_branch = gather_tokens(d_mid.astype(BF))
-    d_attended = dot(d_branch, w_out, NT).astype(BF)
-    grad_output = dot(attended, d_branch, TN).astype(BF)
-    d_lin, sum_query, sum_key = attend_back(
-        lin, d_attended, cosine, sine, gq, gk, nat, seqs, heads, block
-    )
-    grad_qkv = dot(h1, d_lin, TN).astype(BF)
-    d_h1_part = dot(d_lin, w_qkv, NT)
-    sum_attn = jnp.sum(d_h1_part * x_unit, axis=0)
-    d_h1 = scatter_tokens(d_h1_part.astype(BF))
-    own_unit, own_scale = unit_rows(x_own)
-    grad_tokens = d_mid + norm_back(d_h1, ga, own_unit, own_scale)
-
-    def columns_grad(partial):
-        return shard_of_columns(scatter_blocks(partial.reshape(Z, A, -1, partial.shape[-1])))
-
-    def hidden_grad(partial):
-        whole = columns_grad(partial).reshape(shard_rows, Y, C, ZA, down_rows)
+
+    def columns_grad(total):
+        return shard_of_columns(total)
+
+    def hidden_grad(total):
+        whole = shard_of_columns(total).reshape(shard_rows, Y, C, ZA, down_rows)
         return whole.transpose(0, 3, 2, 1, 4).reshape(shard_rows, hidden_units)
 
     def y_copies(own):
@@ -484,24 +904,187 @@
             whole = lax.dynamic_update_slice(whole, held[None].astype(F32), ((y - k) % Y, 0, 0))
         return whole.reshape(-1, own.shape[-1])
 
-    g_down = y_copies(scatter_blocks(grad_down.reshape(Z, A, down_rows, width)))
-    g_gate = hidden_grad(grad_gate)
-    g_up = hidden_grad(grad_up)
-    g_out = scatter_blocks(grad_output.reshape(Z, A, -1, width)).astype(BF)
-    g_out = y_copies(grid.permute(g_out, out_source))
-    g_qkv = columns_grad(grad_qkv).reshape(shard_rows, KV_HEADS, (GROUP + 2) * HEAD_DIM)
+    def term(partial, i, j):
+        at = ((z + i) % Z, (a + j) % A) + (0,) * (partial.ndim - 2)
+        return lax.dynamic_slice(partial, at, (1, 1) + partial.shape[2:])[0, 0]
+
+    def meet(*values):
+        return lax.optimization_barrier(values)
+
+    class Scatter:
+        def __init__(self, partial):
+            self.partial = partial
+            self.over_a = {}
+            self.at = Z - 1
+            self.held = None
+
+        def first(self, i):
+            return term(self.partial, i, A - 1), dict(a=1)
+
+        def got_first(self, i, held):
+            for k in range(1, A):
+                total = held.astype(F32) + term(self.partial, i, A - 1 - k).astype(F32)
+                if k < A - 1:
+                    held = send(total.astype(BF), a=1)
+            self.over_a[i] = total
+            if i == Z - 1:
+                self.total = total
+
+        def hop(self):
+            return self.total.astype(BF), dict(z=1)
+
+        def got_hop(self, held):
+            self.at -= 1
+            self.total = held.astype(F32) + self.over_a[self.at]
+
+    def fly(sends, *values):
+        arrays = [v for v, _ in sends]
+        out = lax.optimization_barrier((*values, *arrays))
+        values, arrays = out[: len(values)], out[len(values) :]
+        return values, [send(v, **to) for v, (_, to) in zip(arrays, sends)]
+
+    r_down = Scatter(grad_down.reshape(Z, A, down_rows, width))
+    (dy2, w_d2), got = fly([r_down.first(3), r_down.first(2)], dy, w_d)
+    d_hidden = dot(dy2, w_d2, NT)
+    d_gate = (d_hidden * gate_factor.astype(F32)).astype(BF)
+    d_upper = (d_hidden * upper_factor.astype(F32)).astype(BF)
+    d_gate, d_upper, *got = meet(d_gate, d_upper, *got)
+    r_down.got_first(3, got[0])
+    r_down.got_first(2, got[1])
+    (d_gate, d_upper), got = fly([r_down.first(1), r_down.first(0), r_down.hop()], d_gate, d_upper)
+    d_h2_part = (dot(d_gate, w_g, NT) + dot(d_upper, w_u, NT)).astype(BF)
+    d_h2_part, *got = meet(d_h2_part, *got)
+    r_down.got_first(1, got[0])
+    r_down.got_first(0, got[1])
+    r_down.got_hop(got[2])
+    parts = d_h2_part.reshape(C, Y, rows, width)
+    other = [(parts[1, j], dict(c=1)) for j in range(Y)] if C == 2 else []
+    (h2_4, d_gate4), got = fly([*other, r_down.hop()], h2, d_gate)
+    grad_gate = dot(h2_4, d_gate4, TN).astype(BF)
+    grad_gate, *got = meet(grad_gate, *got)
+    r_down.got_hop(got[-1])
+    r_gate = Scatter(grad_gate.reshape(Z, A, -1, grad_gate.shape[-1]))
+    summed = [parts[0, j].astype(F32) + (got[j].astype(F32) if C == 2 else 0.0) for j in range(Y)]
+    (h2_5, d_upper5), got = fly(
+        [(summed[Y - 1].astype(BF), dict(y=1)), r_gate.first(3), r_gate.first(2), r_down.hop()], h2, d_upper
+    )
+    grad_up = dot(h2_5, d_upper5, TN).astype(BF)
+    grad_up, *got = meet(grad_up, *got)
+    r_gate.got_first(3, got[1])
+    r_gate.got_first(2, got[2])
+    r_down.got_hop(got[3])
+    r_up = Scatter(grad_up.reshape(Z, A, -1, grad_up.shape[-1]))
+    d_h2 = got[0].astype(F32) + summed[max(Y - 2, 0)]
+    for k in range(2, Y):
+        d_h2 = send(d_h2.astype(BF), y=1).astype(F32) + summed[Y - 1 - k]
+    sum_mlp = jnp.sum(d_h2 * mid_unit, axis=0)
+    d_mid = cotangent.reshape(rows, width).astype(F32) + norm_back(d_h2, gm, mid_unit, mid_scale)
+    d_mid_low = d_mid.astype(BF)
+    (hidden6, w_d6), got = fly([(d_mid_low, dict(y=1)), r_gate.first(1), r_gate.first(0), r_gate.hop()], hidden, w_d)
+    out_part = dot(hidden6, w_d6).astype(BF)
+    out_part, *got = meet(out_part, *got)
+    r_gate.got_first(1, got[1])
+    r_gate.got_first(0, got[2])
+    r_gate.got_hop(got[3])
+    chunks = [None] * Y
+    chunks[0], chunks[Y - 1] = d_mid_low, got[0]
+    for k in range(2, Y):
+        chunks[Y - k] = send(chunks[Y - k + 1], y=1)
+    other = [(chunk, dict(c=1)) for chunk in chunks] if C == 2 else []
+    out_parts = out_part.reshape(C, Y, rows, width)
+    out_other = [(out_parts[1, j], dict(c=1)) for j in range(Y)] if C == 2 else []
+    _, got = fly([*other, *out_other, r_up.first(3), r_gate.hop()])
+    got = meet(*got)
+    r_up.got_first(3, got[-2])
+    r_gate.got_hop(got[-1])
+    d_branch = jnp.concatenate([*chunks, *got[: len(other)]], axis=0)
+    got = got[len(other) :]
+    out_sum = [
+        out_parts[0, j].astype(F32) + (got[j].astype(F32) if C == 2 else 0.0) for j in range(Y)
+    ]
+    (d_branch, w_out8), got = fly(
+        [(out_sum[Y - 1].astype(BF), dict(y=1)), r_up.first(2), r_gate.hop(), r_up.hop()], d_branch, w_out
+    )
+    d_attended = dot(d_branch, w_out8, NT).astype(BF)
+    d_lin, sum_query, sum_key = attend_back(
+        lin, d_attended, cosine, sine, gq, gk, nat, seqs, heads, block
+    )
+    d_lin, *got = meet(d_lin, *got)
+    out_total = got[0].astype(F32) + out_sum[max(Y - 2, 0)]
+    for k in range(2, Y):
+        out_total = send(out_total.astype(BF), y=1).astype(F32) + out_sum[Y - 1 - k]
+    output = x_mid + out_total
+    r_up.got_first(2, got[1])
+    r_gate.got_hop(got[2])
+    r_up.got_hop(got[3])
+    (d_lin, w_qkv9), got = fly([r_up.first(1), r_up.first(0)], d_lin, w_qkv)
+    d_h1_part = dot(d_lin, w_qkv9, NT)
+    sum_attn = jnp.sum(d_h1_part * x_unit, axis=0)
+    d_h1_low, d_lin, *got = meet(d_h1_part.astype(BF), d_lin, *got)
+    r_up.got_first(1, got[0])
+    r_up.got_first(0, got[1])
+    parts = d_h1_low.reshape(C, Y, rows, width)
+    other = [(parts[1, j], dict(c=1)) for j in range(Y)] if C == 2 else []
+    (h1_10, d_lin), got = fly([*other, r_up.hop()], h1, d_lin)
+    grad_qkv = dot(h1_10, d_lin, TN).astype(BF)
+    grad_qkv, *got = meet(grad_qkv, *got)
+    r_up.got_hop(got[-1])
+    summed = [parts[0, j].astype(F32) + (got[j].astype(F32) if C == 2 else 0.0) for j in range(Y)]
+    cut = [sum_attn.reshape(ZA * C, n), sum_mlp.reshape(ZA * C, n)]
+    cut += [sum_query[0].reshape(ZA * C, m), sum_key[0].reshape(ZA * C, m)]
+    sums = jnp.concatenate(cut, axis=1)
+    sums = jnp.pad(sums, ((0, 0), (0, 8 * qkv_width - sums.shape[1]))).reshape(ZA * C, 8, qkv_width)
+    r_qkv = Scatter(
+        jnp.concatenate([grad_qkv.reshape(ZA * C, -1, qkv_width), sums.astype(BF)], axis=1).reshape(
+            Z, A, -1, qkv_width
+        )
+    )
+    (attended11, d_branch11), got = fly(
+        [(summed[Y - 1].astype(BF), dict(y=1)), r_qkv.first(3), r_qkv.first(2), r_up.hop()], attended, d_branch
+    )
+    grad_output = dot(attended11, d_branch11, TN).astype(BF)
+    grad_output, *got = meet(grad_output, *got)
+    d_h1 = got[0].astype(F32) + summed[max(Y - 2, 0)]
+    for k in range(2, Y):
+        d_h1 = send(d_h1.astype(BF), y=1).astype(F32) + summed[Y - 1 - k]
+    r_qkv.got_first(3, got[1])
+    r_qkv.got_first(2, got[2])
+    r_up.got_hop(got[3])
+    r_out = Scatter(grad_output.reshape(Z, A, -1, width))
+    own_unit, own_scale = unit_rows(x_own)
+    grad_tokens = d_mid + norm_back(d_h1, ga, own_unit, own_scale)
+    _, got = fly([r_qkv.first(1), r_qkv.hop(), r_out.first(3), r_out.first(2)])
+    got = meet(*got)
+    r_qkv.got_first(1, got[0])
+    r_qkv.got_hop(got[1])
+    r_out.got_first(3, got[2])
+    r_out.got_first(2, got[3])
+    _, got = fly([r_qkv.first(0), r_qkv.hop(), r_out.hop(), r_out.first(1)])
+    got = meet(*got)
+    r_qkv.got_first(0, got[0])
+    r_qkv.got_hop(got[1])
+    r_out.got_first(1, got[3])
+    r_out.got_hop(got[2])
+    _, got = fly([r_out.first(0), r_qkv.hop(), r_out.hop()])
+    got = meet(*got)
+    r_out.got_first(0, got[0])
+    r_qkv.got_hop(got[1])
+    r_out.got_hop(got[2])
+    r_out.got_hop(send(*r_out.hop()[:1], z=1))
+
+    g_down = y_copies(r_down.total)
+    g_gate = hidden_grad(r_gate.total)
+    g_up = hidden_grad(r_up.total)
+    whole_qkv = columns_grad(r_qkv.total)
+    sums = whole_qkv[shard_rows:].sum((1, 2)).reshape(-1)
+    s_attn, s_mlp = sums[:n], sums[n : 2 * n]
+    s_query, s_key = sums[2 * n : 2 * n + m], sums[2 * n + m : 2 * n + 2 * m]
+    g_qkv = whole_qkv[:shard_rows].reshape(shard_rows, KV_HEADS, (GROUP + 2) * HEAD_DIM)
+    g_out = y_copies(grid.permute(r_out.total.astype(BF), out_source))
     g_query = g_qkv[:, :, : GROUP * HEAD_DIM].reshape(shard_rows, -1)
     g_key = g_qkv[:, :, GROUP * HEAD_DIM : (GROUP + 1) * HEAD_DIM].reshape(shard_rows, -1)
     g_value = g_qkv[:, :, (GROUP + 1) * HEAD_DIM :].reshape(shard_rows, -1)
 
-    sums = lax.psum(
-        jnp.concatenate([sum_attn, sum_mlp, sum_query[0], sum_key[0]]), AXES
-    )
-    shard = (z * A + a) * C + c
-    s_attn = lax.dynamic_slice_in_dim(sums, shard * n, n)
-    s_mlp = lax.dynamic_slice_in_dim(sums, width + shard * n, n)
-    s_query = lax.dynamic_slice_in_dim(sums, 2 * width + shard * m, m)
-    s_key = lax.dynamic_slice_in_dim(sums, 2 * width + HEAD_DIM + shard * m, m)
     return (
         output.astype(BF).reshape(tokens.shape), grad_tokens.astype(BF).reshape(tokens.shape),
         g_query, g_key, g_value, g_out, g_gate, g_up, g_down, s_attn, s_mlp, s_query, s_key,

time: 1230 us -> 1070 us (0.87); the launches traced: 1210 us -> 1070 us
  waiting for transfers between devices: 530 us -> 221 us
  Pallas kernels: 57.6 us -> 310 us
  blocking collectives: 43.5 us -> 0 us
  local copies, waits for them, and re-layouts: 144 us -> 109 us
  starting transfers between devices: 96.8 us -> 66.1 us
  other arithmetic: 87.3 us -> 113 us
    ppermute x110 -> x60, waiting for transfers between devices: 530 us -> 221 us  [permute(): return lax.ppermute(value, AXES, pairs)]
    pallas_call x0 -> x2, Pallas kernels: none -> 252 us  [the longest x1 131 us: join(): pl.pallas_call(functools.partial(join_kernel, grid, halves, weights_progr...]
    psum x1 -> x0, blocking collectives: 43.5 us -> none  [on_device(): lax.psum(jnp.concatenate([sum_attn, sum_mlp, sum_query[0], sum_key[0]]),...]
    ppermute x110 -> x60, starting transfers between devices: 96.8 us -> 66.1 us  [permute(): return lax.ppermute(value, AXES, pairs)]
    dynamic_update_slice x37 -> x1, local copies, waits for them, and re-layouts: 24.6 us -> 2.33 us  [on_device(): lax.dynamic_update_slice(down_all, side[:, None], (0, (a - k) % A, 0, 0))]
    unnamed x135 -> x153, local copies, waits for them, and re-layouts: 36.1 us -> 50.6 us
    convert_element_type x22 -> x21, other arithmetic: 39.6 us -> 53.9 us  [the longest x15 28.2 us: hop(): return (self.total.astype(BF), dict(z=1))]
  transfers between devices with their start and end apart: 110 -> 60, of which waited for: 50 -> 22; matrix products, arithmetic and copies ran while one was open for 32% -> 28% of each run, Pallas kernels for 2% -> 3%
where the time goes in v2:
time: 1070 us
  Pallas kernels  310 us (29%)
  matrix products  248 us (23%)
  waiting for transfers between devices  221 us (21%)
  other arithmetic  113 us (11%)
  local copies, waits for them, and re-layouts  109 us (10%)
  starting transfers between devices  66.1 us (6%)
    dot_general x15, matrix products, dot(): lax.dot_general(left, right, (dims, ((), ())), preferred_element_type=F32)  248 us
    ppermute x60, waiting for transfers between devices, permute(): return lax.ppermute(value, AXES, pairs)  221 us
    pallas_call x1, Pallas kernels, join(): pl.pallas_call(functools.partial(join_kernel, grid, halves, weights_progr...  131 us
    pallas_call x1, Pallas kernels, gather_start(): pl.pallas_call(functools.partial(gather_start_kernel, grid, *targets), ou...  122 us
    ppermute x60, starting transfers between devices, permute(): return lax.ppermute(value, AXES, pairs)  66.1 us
    unnamed x153, local copies, waits for them, and re-layouts  50.6 us
    pallas_call x1, Pallas kernels, attend_back(): pl.pallas_call(functools.partial(attend_back_kernel, block, blocks, tile)...  36.4 us
    convert_element_type x15, other arithmetic, hop(): return (self.total.astype(BF), dict(z=1))  28.2 us
  transfers between devices with their start and end apart: 60, of which 22 were waited for; matrix products, arithmetic and copies ran while one was open for 28% of the time, Pallas kernels for 3%

profile of v2, /device:TPU:0, one launch (start us, length us, event | category | flops | bytes accessed | tf_op | source)
XLA Modules:
  0.0 1068.8 jit_solution(17983891626895851401)
XLA Ops:
  24.0 121.6 %gather_start.1 = (bf16[2,2,512,2048]{3,2,1,0:T(8,128)(2,1)}, s32[2,2,4,128]{3,2,1,0:T(4,128)S(1)}, bf16[4,2,2,128,1024]{4,3,2,1,0:T(8,128)(2,1)S(1)}, bf16[4,2,...) custom-call(bf16[512,2048]{1,0:T(8,128)(2,1)S(1)} %bitcast.363, ...), custom_call_target="tpu_custom_call" | custom-call | bytes 300000000 | tf_op jit(solution)/shard_map/gather_start/pallas_call | solution.py:661
  179.6 14.5 %fusion.93.lin_ref = f32[2048,1024]{1,0:T(8,128)} fusion(bf16[2048,2048]{1,0:T(8,128)(2,1)} %bitcast.401, bf16[2048,1024]{1,0:T(8,128)(2,1)} %bitcast.374), kind=kOutput, calls=%fused_computation.247 | convolution fusion | flops 8589934592 | bytes 20971520 | tf_op jit(solution)/shard_map/dot_general | solution.py:24
  195.4 21.0 %attend.1 = bf16[2048,512]{1,0:T(8,128)(2,1)} custom-call(s32[4]{0:T(128)} %select_n.419.nat_ref, f32[2048,1024]{1,0:T(8,128)} %fusion.93.lin_ref, f32[2048,128]{1,0:T(8,128)} %pad_maximum_fusion.3.cos_ref, f32[2048,128]{1,0:T(8,128)} %pad_maximum_fusion.4.sin_ref, f32[1,128]{1,0:T(1,128)} %reshape.573.gq_ref, f32[1,128]{1,0:T(1,128)} %reshape.574.gk_ref), custom_call_target="tpu_custom_call" | custom-call | flops 3221225472 | bytes 8388608 | tf_op jit(solution)/shard_map/attend/pallas_call | solution.py:175
  225.0 130.7 %join.1 = (f32[512,2048]{1,0:T(8,128)S(1)}, bf16[2,2,512,2048]{3,2,1,0:T(8,128)(2,1)}, bf16[4,2,2,128,1536]{4,3,2,1,0:T(8,128)(2,1)S(1)}, bf16[4,2,2,128,1536]{4,3,2,1,0:T(8,128)(2,1)}, bf16[4,2,192,2048]{3,2,1,0:T(8,128)(2,1)}) custom-call(bf16[2,2,512,2048]{3,2,1,0:T(8,128)(2,1)} %bitcast.407, ...), custom_call_target="tpu_custom_call", output_to_operand_aliasing={{2}: (3, {}), {3}: (4, {}), {4}: (5, {})} | custom-call | bytes 300000000 | tf_op jit(solution)/shard_map/join/pallas_call | solution.py:680
  360.3 12.9 %collective-permute-start = (bf16[512,2048]{1,0:T(8,128)(2,1)}, bf16[512,2048]{1,0:T(8,128)(2,1)}, u32[]{:S(2)}, u32[]{:S(2)}) collective-permute-start(bf16[512,2048]{1,0:T(8,128)(2,1)} %bitcast.23), channel_id=1, source_target_pairs={{0,4},{1,5},{2,6},{3,7},{4,0},{5,1},{6,2},{7,3},{8,12},{9,13},{10,... | collective-permute-start | bytes 6291464 | tf_op jit(solution)/shard_map/ppermute | solution.py:733
  381.4 17.4 %fusion.94 = f32[2048,1536]{1,0:T(8,128)} fusion(bf16[2048,2048]{1,0:T(8,128)(2,1)} %bitcast.460, bf16[2048,1536]{1,0:T(8,128)(2,1)S(1)} %bitcast.368), kind=kOutput, calls=%fused_computation.248 | convolution fusion | flops 12884901888 | bytes 27262976 | tf_op jit(solution)/shard_map/dot_general | solution.py:24
  398.8 14.6 %collective-permute-done = bf16[512,2048]{1,0:T(8,128)(2,1)} collective-permute-done((bf16[512,2048]{1,0:T(8,128)(2,1)}, bf16[512,2048]{1,0:T(8,128)(2,1)}, u32[]{:S(2)}, u32[]{:S(2)}) %collective-permute-start) | collective-permute-done | bytes 2097184 | tf_op jit(solution)/shard_map/ppermute | solution.py:733
  413.5 25.3 %multiply_convert_fusion.5 = (bf16[2048,1536]{1,0:T(8,128)(2,1)}, f32[2048,1536]{1,0:T(8,128)}) fusion(f32[2048,1536]{1,0:T(8,128)} %fusion.94, bf16[2048,2048]{1,0:T(8,128)(2,1)} %bitcast.461, bf16[2048,1536]{1,0:T(8,128)(2,1)} %bitcast.425), kind=kOutput, calls=%fused_computation.10 | convolution fusion | flops 12903776256 | bytes 46137344 | tf_op jit(solution)/shard_map/dot_general | solution.py:24
  456.2 14.7 %convolution_convert_fusion.4 = bf16[1536,2048]{1,0:T(8,128)(2,1)S(1)} fusion(bf16[2048,1536]{1,0:T(8,128)(2,1)S(1)} %bitcast.467, bf16[2048,2048]{1,0:T(8,128)(2,1)S(1)} %constant_dynamic-update-slice_fusion.2), kind=kOutput, calls=%fused_computation.18 | convolution fusion | flops 12888047616 | bytes 20971520 | tf_op jit(solution)/shard_map/dot_general | solution.py:24
  479.5 29.0 %multiply_convert_fusion.2 = (bf16[2048,1536]{1,0:T(8,128)(2,1)}, bf16[2048,1536]{1,0:T(8,128)(2,1)}) fusion(f32[2048,1536]{1,0:T(8,128)} %fusion.94, f32[2048,1536]{1,0:T(8,128)} %get-tuple-element.409, bf16[2048,2048]{1,0:T(8,128)(2,1)} %copy-done.37, bf16[1536,2048]{1,0:T(8,128)(2,1)} %bitcast.383), kind=kOutput, calls=%fused_computation.7 | convolution fusion | flops 12938379264 | bytes 52428800 | tf_op jit(solution)/shard_map/dot_general | solution.py:24
  517.1 19.7 %fusion.95 = f32[2048,2048]{1,0:T(8,128)} fusion(bf16[2048,1536]{1,0:T(8,128)(2,1)} %get-tuple-element.179, bf16[2048,1536]{1,0:T(8,128)(2,1)} %bitcast.367), kind=kOutput, calls=%fused_computation.249 | convolution fusion | flops 12884901888 | bytes 29360128 | tf_op jit(solution)/shard_map/dot_general | solution.py:24
  540.0 21.7 %add_convert_fusion = bf16[2048,2048]{1,0:T(8,128)(2,1)} fusion(f32[2048,2048]{1,0:T(8,128)} %fusion.95, bf16[2048,1536]{1,0:T(8,128)(2,1)} %get-tuple-element.188, bf16[2048,1536]{1,0:T(8,128)(2,1)} %bitcast.426), kind=kOutput, calls=%fused_computation.4 | convolution fusion | flops 12893290496 | bytes 37748736 | tf_op jit(solution)/shard_map/dot_general | solution.py:24
  561.7 11.6 %collective-permute-done.7 = bf16[192,2048]{1,0:T(8,128)(2,1)} collective-permute-done((bf16[192,2048]{1,0:T(8,128)(2,1)S(1)}, bf16[192,2048]{1,0:T(8,128)(2,1)}, u32[]{:S(2)}, u32[]{:S(2)}) %collective-permute-start.7) | collective-permute-done | bytes 786464 | tf_op jit(solution)/shard_map/ppermute | solution.py:733
  579.6 17.5 %convolution_convert_fusion.3 = bf16[2048,1536]{1,0:T(8,128)(2,1)S(1)} fusion(bf16[2048,2048]{1,0:T(8,128)(2,1)} %bitcast.462, bf16[2048,1536]{1,0:T(8,128)(2,1)} %get-tuple-element.179), kind=kOutput, calls=%fused_computation.17 | convolution fusion | flops 12888047616 | bytes 20971520 | tf_op jit(solution)/shard_map/dot_general | solution.py:24
  607.5 19.2 %convolution_convert_fusion.2 = bf16[2048,1536]{1,0:T(8,128)(2,1)} fusion(bf16[2048,2048]{1,0:T(8,128)(2,1)} %bitcast.463, bf16[2048,1536]{1,0:T(8,128)(2,1)} %get-tuple-element.188), kind=kOutput, calls=%fused_computation.16 | convolution fusion | flops 12888047616 | bytes 20971520 | tf_op jit(solution)/shard_map/dot_general | solution.py:24
  626.8 14.0 %collective-permute-done.14 = bf16[256,1536]{1,0:T(8,128)(2,1)S(1)} collective-permute-done((bf16[256,1536]{1,0:T(8,128)(2,1)S(1)}, bf16[256,1536]{1,0:T(8,128)(2,1)S(1)}, u32[]{:S(2)}, u32[]{:S(2)}) %collective-permute-start.14) | collective-permute-done | bytes 786464 | tf_op jit(solution)/shard_map/ppermute | solution.py:733
  663.2 15.6 %convolution_convert_fusion = bf16[2048,2048]{1,0:T(8,128)(2,1)S(1)} fusion(bf16[2048,1536]{1,0:T(8,128)(2,1)} %get-tuple-element.196, bf16[1536,2048]{1,0:T(8,128)(2,1)S(1)} %bitcast.386), kind=kOutput, calls=%fused_computation.14 | convolution fusion | flops 12889096192 | bytes 20971520 | tf_op jit(solution)/shard_map/dot_general | solution.py:24
  684.5 11.2 %collective-permute-done.18 = bf16[256,1536]{1,0:T(8,128)(2,1)S(1)} collective-permute-done((bf16[256,1536]{1,0:T(8,128)(2,1)}, bf16[256,1536]{1,0:T(8,128)(2,1)S(1)}, u32[]{:S(2)}, u32[]{:S(2)}) %collective-permute-start.18) | collective-permute-done | bytes 786464 | tf_op jit(solution)/shard_map/ppermute | solution.py:733
  695.7 9.9 collective-permute-done.16
  712.8 17.9 %collective-permute-done.24 = bf16[256,1536]{1,0:T(8,128)(2,1)S(1)} collective-permute-done((bf16[256,1536]{1,0:T(8,128)(2,1)S(1)}, bf16[256,1536]{1,0:T(8,128)(2,1)S(1)}, u32[]{:S(2)}, u32[]{:S(2)}) %collective-permute-start.24) | collective-permute-done | bytes 786464 | tf_op jit(solution)/shard_map/ppermute | solution.py:733
  737.0 14.5 %collective-permute-done.25 = bf16[256,1536]{1,0:T(8,128)(2,1)} collective-permute-done((bf16[256,1536]{1,0:T(8,128)(2,1)}, bf16[256,1536]{1,0:T(8,128)(2,1)}, u32[]{:S(2)}, u32[]{:S(2)}) %collective-permute-start.25) | collective-permute-done | bytes 786464 | tf_op jit(solution)/shard_map/ppermute | solution.py:733
  779.6 36.4 %attend_back.1 = (bf16[2048,1024]{1,0:T(8,128)(2,1)}, f32[8,128]{1,0:T(8,128)}, f32[8,128]{1,0:T(8,128)}) custom-call(s32[4]{0:T(128)} %select_n.419.nat_ref, f32[2048,1024]{1,0:T(8,128)} %fusion.93.lin_ref, bf16[2048,512]{1,0:T(8,128)(2,1)} %convolution_convert_fusion.7.do_ref, f32[2048,128]{1,0:T(8,128)} %pad_maximum_fusion.3.cos_ref, ...), custom_call_target="tpu_custom_call" | custom-call | flops 7516192768 | bytes 16777216 | tf_op jit(solution)/shard_map/attend_back/pallas_call | solution.py:208
  819.8 18.5 %multiply_reduce_fusion = (bf16[2048]{0:T(1024)(128)(2,1)S(1)}, bf16[2048,2048]{1,0:T(8,128)(2,1)}, bf16[2048,2048]{1,0:T(8,128)(2,1)}) fusion(bf16[2,2,512,2048]{3,2,1,0:T(8,128)(2,1)} %get-tuple-element.150, f32[2048]{0:T(1024)S(1)} %bitcast.458, f32[2048]{0:T(1024)S(1)} %copy-done.43, bf16[2048,1024]{1,0:T(8,128)(2,1)} %get-tuple-element.238, ...), kind=kOutput, calls=%fused_computation.2 | convolution fusion | flops 8619292672 | bytes 33574912 | tf_op jit(solution)/shard_map/dot_general | solution.py:24
  857.7 10.0 convolution_convert_fusion.5
  867.7 10.8 %collective-permute-done.34 = bf16[256,1536]{1,0:T(8,128)(2,1)S(1)} collective-permute-done((bf16[256,1536]{1,0:T(8,128)(2,1)S(1)}, bf16[256,1536]{1,0:T(8,128)(2,1)S(1)}, u32[]{:S(2)}, u32[]{:S(2)}) %collective-permute-start.34) | collective-permute-done | bytes 786464 | tf_op jit(solution)/shard_map/ppermute | solution.py:733
  896.7 9.9 convolution_convert_fusion.6
  910.5 10.2 collective-permute-done.37
  920.7 14.8 %collective-permute-done.35 = bf16[512,2048]{1,0:T(8,128)(2,1)} collective-permute-done((bf16[512,2048]{1,0:T(8,128)(2,1)}, bf16[512,2048]{1,0:T(8,128)(2,1)}, u32[]{:S(2)}, u32[]{:S(2)}) %collective-permute-start.35) | collective-permute-done | bytes 2097184 | tf_op jit(solution)/shard_map/ppermute | solution.py:733
  954.3 9.8 collective-permute-done.41
  978.5 15.2 %collective-permute-done.45 = bf16[64,2048]{1,0:T(8,128)(2,1)S(1)} collective-permute-done((bf16[64,2048]{1,0:T(8,128)(2,1)S(1)}, bf16[64,2048]{1,0:T(8,128)(2,1)S(1)}, u32[]{:S(2)}, u32[]{:S(2)}) %collective-permute-start.45) | collective-permute-done | bytes 262176 | tf_op jit(solution)/shard_map/ppermute | solution.py:733
  1005.6 12.2 %collective-permute-done.49 = bf16[64,2048]{1,0:T(8,128)(2,1)S(1)} collective-permute-done((bf16[64,2048]{1,0:T(8,128)(2,1)S(1)}, bf16[64,2048]{1,0:T(8,128)(2,1)S(1)}, u32[]{:S(2)}, u32[]{:S(2)}) %collective-permute-start.49) | collective-permute-done | bytes 262176 | tf_op jit(solution)/shard_map/ppermute | solution.py:733
  1040.3 14.5 %collective-permute-done.54 = bf16[64,2048]{1,0:T(8,128)(2,1)S(1)} collective-permute-done((bf16[64,2048]{1,0:T(8,128)(2,1)S(1)}, bf16[64,2048]{1,0:T(8,128)(2,1)S(1)}, u32[]{:S(2)}, u32[]{:S(2)}) %collective-permute-start.54) | collective-permute-done | bytes 262176 | tf_op jit(solution)/shard_map/ppermute | solution.py:733
  (385 shorter events, 329.8 us)
Async XLA Ops:
  360.3 53.2 %collective-permute-start = (bf16[512,2048]{1,0:T(8,128)(2,1)}, bf16[512,2048]{1,0:T(8,128)(2,1)}, u32[]{:S(2)}, u32[]{:S(2)}) collective-permute-start(bf16[512,2048]{1,0:T(8,128)(2,1)} %bitcast.23), channel_id=1, source_target_pairs={{0,4},{1,5},{2,6},{3,7},{4,0},{5,1},{6,2},{7,3},{8,12},{9,13},{10,... | collective-permute-start | bytes 6291464 | tf_op jit(solution)/shard_map/ppermute | solution.py:733
  373.2 72.4 %collective-permute-start.1 = (bf16[512,2048]{1,0:T(8,128)(2,1)}, bf16[512,2048]{1,0:T(8,128)(2,1)}, u32[]{:S(2)}, u32[]{:S(2)}) collective-permute-start(bf16[512,2048]{1,0:T(8,128)(2,1)} %bitcast.23), channel_id=1, source_target_pairs={{0,1},{1,0},{2,3},{3,2},{4,5},{5,4},{6,7},{7,6},{8,9},{9,8},{10,11... | collective-permute-start | bytes 6291464 | tf_op jit(solution)/shard_map/ppermute | solution.py:733
  377.3 73.2 %collective-permute-start.3 = (bf16[4,192,2048]{2,1,0:T(8,128)(2,1)}, bf16[4,192,2048]{2,1,0:T(8,128)(2,1)}, u32[]{:S(2)}, u32[]{:S(2)}) collective-permute-start(bf16[4,192,2048]{2,1,0:T(8,128)(2,1)} %dynamic-slice_bitcast_fusion), channel_id=1, source_target_pairs={{0,2},{1,3},{2,0},{3,1},{4,6},{5,7},{6,4},{7,5},{8,10},{9,11},{10,... | collective-permute-start | bytes 9437192 | tf_op jit(solution)/shard_map/ppermute | solution.py:733
  413.5 39.4 %collective-permute-start.2 = (bf16[512,2048]{1,0:T(8,128)(2,1)}, bf16[512,2048]{1,0:T(8,128)(2,1)}, u32[]{:S(2)}, u32[]{:S(2)}) collective-permute-start(bf16[512,2048]{1,0:T(8,128)(2,1)} %collective-permute-done), channel_id=1, source_target_pairs={{0,1},{1,0},{2,3},{3,2},{4,5},{5,4},{6,7},{7,6},{8,9},{9,8},{10,11... | collective-permute-start | bytes 6291464 | tf_op jit(solution)/shard_map/ppermute | solution.py:733
  474.7 33.8 %collective-permute-start.4 = (bf16[192,2048]{1,0:T(8,128)(2,1)S(1)}, bf16[192,2048]{1,0:T(8,128)(2,1)S(1)}, u32[]{:S(2)}, u32[]{:S(2)}) collective-permute-start(bf16[192,2048]{1,0:T(8,128)(2,1)S(1)} %get-tuple-element.165), channel_id=1, source_target_pairs={{0,2},{1,3},{2,0},{3,1},{4,6},{5,7},{6,4},{7,5},{8,10},{9,11},{10,... | collective-permute-start | bytes 2359304 | tf_op jit(solution)/shard_map/ppermute | solution.py:733
  479.5 35.0 %collective-permute-start.5 = (bf16[192,2048]{1,0:T(8,128)(2,1)S(1)}, bf16[192,2048]{1,0:T(8,128)(2,1)S(1)}, u32[]{:S(2)}, u32[]{:S(2)}) collective-permute-start(bf16[192,2048]{1,0:T(8,128)(2,1)S(1)} %get-tuple-element.166), channel_id=1, source_target_pairs={{0,2},{1,3},{2,0},{3,1},{4,6},{5,7},{6,4},{7,5},{8,10},{9,11},{10,... | collective-permute-start | bytes 2359304 | tf_op jit(solution)/shard_map/ppermute | solution.py:733
  538.5 34.8 %collective-permute-start.7 = (bf16[192,2048]{1,0:T(8,128)(2,1)S(1)}, bf16[192,2048]{1,0:T(8,128)(2,1)}, u32[]{:S(2)}, u32[]{:S(2)}) collective-permute-start(bf16[192,2048]{1,0:T(8,128)(2,1)S(1)} %get-tuple-element.173), channel_id=1, source_target_pairs={{0,2},{1,3},{2,0},{3,1},{4,6},{5,7},{6,4},{7,5},{8,10},{9,11},{10,... | collective-permute-start | bytes 2359304 | tf_op jit(solution)/shard_map/ppermute | solution.py:733
  538.8 34.5 %collective-permute-start.8 = (bf16[192,2048]{1,0:T(8,128)(2,1)}, bf16[192,2048]{1,0:T(8,128)(2,1)}, u32[]{:S(2)}, u32[]{:S(2)}) collective-permute-start(bf16[192,2048]{1,0:T(8,128)(2,1)} %fusion.40), channel_id=1, source_target_pairs={{0,8},{1,9},{2,10},{3,11},{4,12},{5,13},{6,14},{7,15},{8,16},{9,17... | collective-permute-start | bytes 2359304 | tf_op jit(solution)/shard_map/ppermute | solution.py:733
  603.7 46.8 %collective-permute-start.12 = (bf16[512,2048]{1,0:T(8,128)(2,1)S(1)}, bf16[512,2048]{1,0:T(8,128)(2,1)S(1)}, u32[]{:S(2)}, u32[]{:S(2)}) collective-permute-start(bf16[512,2048]{1,0:T(8,128)(2,1)S(1)} %fusion.17), channel_id=1, source_target_pairs={{0,4},{1,5},{2,6},{3,7},{4,0},{5,1},{6,2},{7,3},{8,12},{9,13},{10,... | collective-permute-start | bytes 6291464 | tf_op jit(solution)/shard_map/ppermute | solution.py:733
  607.0 33.7 %collective-permute-start.14 = (bf16[256,1536]{1,0:T(8,128)(2,1)S(1)}, bf16[256,1536]{1,0:T(8,128)(2,1)S(1)}, u32[]{:S(2)}, u32[]{:S(2)}) collective-permute-start(bf16[256,1536]{1,0:T(8,128)(2,1)S(1)} %get-tuple-element.191), channel_id=1, source_target_pairs={{0,2},{1,3},{2,0},{3,1},{4,6},{5,7},{6,4},{7,5},{8,10},{9,11},{10,... | collective-permute-start | bytes 2359304 | tf_op jit(solution)/shard_map/ppermute | solution.py:733
  607.5 33.2 %collective-permute-start.15 = (bf16[192,2048]{1,0:T(8,128)(2,1)S(1)}, bf16[192,2048]{1,0:T(8,128)(2,1)S(1)}, u32[]{:S(2)}, u32[]{:S(2)}) collective-permute-start(bf16[192,2048]{1,0:T(8,128)(2,1)S(1)} %fusion.37), channel_id=1, source_target_pairs={{0,8},{1,9},{2,10},{3,11},{4,12},{5,13},{6,14},{7,15},{8,16},{9,17... | collective-permute-start | bytes 2359304 | tf_op jit(solution)/shard_map/ppermute | solution.py:733
  659.4 46.2 %collective-permute-start.16 = (bf16[512,2048]{1,0:T(8,128)(2,1)}, bf16[512,2048]{1,0:T(8,128)(2,1)}, u32[]{:S(2)}, u32[]{:S(2)}) collective-permute-start(bf16[512,2048]{1,0:T(8,128)(2,1)} %get-tuple-element.207), channel_id=1, source_target_pairs={{0,4},{1,5},{2,6},{3,7},{4,0},{5,1},{6,2},{7,3},{8,12},{9,13},{10,... | collective-permute-start | bytes 6291464 | tf_op jit(solution)/shard_map/ppermute | solution.py:733
  662.7 33.0 %collective-permute-start.18 = (bf16[256,1536]{1,0:T(8,128)(2,1)}, bf16[256,1536]{1,0:T(8,128)(2,1)S(1)}, u32[]{:S(2)}, u32[]{:S(2)}) collective-permute-start(bf16[256,1536]{1,0:T(8,128)(2,1)} %get-tuple-element.200), channel_id=1, source_target_pairs={{0,2},{1,3},{2,0},{3,1},{4,6},{5,7},{6,4},{7,5},{8,10},{9,11},{10,... | collective-permute-start | bytes 2359304 | tf_op jit(solution)/shard_map/ppermute | solution.py:733
  663.2 32.5 %collective-permute-start.19 = (bf16[256,1536]{1,0:T(8,128)(2,1)}, bf16[256,1536]{1,0:T(8,128)(2,1)}, u32[]{:S(2)}, u32[]{:S(2)}) collective-permute-start(bf16[256,1536]{1,0:T(8,128)(2,1)} %fusion.35), channel_id=1, source_target_pairs={{0,8},{1,9},{2,10},{3,11},{4,12},{5,13},{6,14},{7,15},{8,16},{9,17... | collective-permute-start | bytes 2359304 | tf_op jit(solution)/shard_map/ppermute | solution.py:733
  710.3 42.9 %collective-permute-start.20 = (bf16[512,2048]{1,0:T(8,128)(2,1)}, bf16[512,2048]{1,0:T(8,128)(2,1)}, u32[]{:S(2)}, u32[]{:S(2)}) collective-permute-start(bf16[512,2048]{1,0:T(8,128)(2,1)} %get-tuple-element.207), channel_id=1, source_target_pairs={{0,1},{1,0},{2,3},{3,2},{4,5},{5,4},{6,7},{7,6},{8,9},{9,8},{10,11... | collective-permute-start | bytes 6291464 | tf_op jit(solution)/shard_map/ppermute | solution.py:733
  710.3 42.9 %collective-permute-start.21 = (bf16[512,2048]{1,0:T(8,128)(2,1)}, bf16[512,2048]{1,0:T(8,128)(2,1)}, u32[]{:S(2)}, u32[]{:S(2)}) collective-permute-start(bf16[512,2048]{1,0:T(8,128)(2,1)} %collective-permute-done.16), channel_id=1, source_target_pairs={{0,1},{1,0},{2,3},{3,2},{4,5},{5,4},{6,7},{7,6},{8,9},{9,8},{10,11... | collective-permute-start | bytes 6291464 | tf_op jit(solution)/shard_map/ppermute | solution.py:733
  710.8 42.4 %collective-permute-start.22 = (bf16[512,2048]{1,0:T(8,128)(2,1)}, bf16[512,2048]{1,0:T(8,128)(2,1)}, u32[]{:S(2)}, u32[]{:S(2)}) collective-permute-start(bf16[512,2048]{1,0:T(8,128)(2,1)} %get-tuple-element.209), channel_id=1, source_target_pairs={{0,1},{1,0},{2,3},{3,2},{4,5},{5,4},{6,7},{7,6},{8,9},{9,8},{10,11... | collective-permute-start | bytes 6291464 | tf_op jit(solution)/shard_map/ppermute | solution.py:733
  710.8 42.4 %collective-permute-start.23 = (bf16[512,2048]{1,0:T(8,128)(2,1)}, bf16[512,2048]{1,0:T(8,128)(2,1)}, u32[]{:S(2)}, u32[]{:S(2)}) collective-permute-start(bf16[512,2048]{1,0:T(8,128)(2,1)} %get-tuple-element.210), channel_id=1, source_target_pairs={{0,1},{1,0},{2,3},{3,2},{4,5},{5,4},{6,7},{7,6},{8,9},{9,8},{10,11... | collective-permute-start | bytes 6291464 | tf_op jit(solution)/shard_map/ppermute | solution.py:733
  767.4 50.2 %collective-permute-start.26 = (bf16[512,2048]{1,0:T(8,128)(2,1)}, bf16[512,2048]{1,0:T(8,128)(2,1)}, u32[]{:S(2)}, u32[]{:S(2)}) collective-permute-start(bf16[512,2048]{1,0:T(8,128)(2,1)} %fusion.15), channel_id=1, source_target_pairs={{0,4},{1,5},{2,6},{3,7},{4,0},{5,1},{6,2},{7,3},{8,12},{9,13},{10,... | collective-permute-start | bytes 6291464 | tf_op jit(solution)/shard_map/ppermute | solution.py:733
  771.9 45.7 %collective-permute-start.27 = (bf16[256,1536]{1,0:T(8,128)(2,1)S(1)}, bf16[256,1536]{1,0:T(8,128)(2,1)}, u32[]{:S(2)}, u32[]{:S(2)}) collective-permute-start(bf16[256,1536]{1,0:T(8,128)(2,1)S(1)} %copy-done.27), channel_id=1, source_target_pairs={{0,2},{1,3},{2,0},{3,1},{4,6},{5,7},{6,4},{7,5},{8,10},{9,11},{10,... | collective-permute-start | bytes 2359304 | tf_op jit(solution)/shard_map/ppermute | solution.py:733
  773.4 44.2 %collective-permute-start.28 = (bf16[256,1536]{1,0:T(8,128)(2,1)}, bf16[256,1536]{1,0:T(8,128)(2,1)}, u32[]{:S(2)}, u32[]{:S(2)}) collective-permute-start(bf16[256,1536]{1,0:T(8,128)(2,1)} %fusion.32), channel_id=1, source_target_pairs={{0,8},{1,9},{2,10},{3,11},{4,12},{5,13},{6,14},{7,15},{8,16},{9,17... | collective-permute-start | bytes 2359304 | tf_op jit(solution)/shard_map/ppermute | solution.py:733
  773.5 44.2 %collective-permute-start.29 = (bf16[256,1536]{1,0:T(8,128)(2,1)}, bf16[256,1536]{1,0:T(8,128)(2,1)}, u32[]{:S(2)}, u32[]{:S(2)}) collective-permute-start(bf16[256,1536]{1,0:T(8,128)(2,1)} %fusion.30), channel_id=1, source_target_pairs={{0,8},{1,9},{2,10},{3,11},{4,12},{5,13},{6,14},{7,15},{8,16},{9,17... | collective-permute-start | bytes 2359304 | tf_op jit(solution)/shard_map/ppermute | solution.py:733
  817.7 33.1 %collective-permute-start.30 = (bf16[256,1536]{1,0:T(8,128)(2,1)}, bf16[256,1536]{1,0:T(8,128)(2,1)}, u32[]{:S(2)}, u32[]{:S(2)}) collective-permute-start(bf16[256,1536]{1,0:T(8,128)(2,1)} %get-tuple-element.231), channel_id=1, source_target_pairs={{0,2},{1,3},{2,0},{3,1},{4,6},{5,7},{6,4},{7,5},{8,10},{9,11},{10,... | collective-permute-start | bytes 2359304 | tf_op jit(solution)/shard_map/ppermute | solution.py:733
  818.2 32.5 %collective-permute-start.31 = (bf16[256,1536]{1,0:T(8,128)(2,1)}, bf16[256,1536]{1,0:T(8,128)(2,1)}, u32[]{:S(2)}, u32[]{:S(2)}) collective-permute-start(bf16[256,1536]{1,0:T(8,128)(2,1)} %get-tuple-element.232), channel_id=1, source_target_pairs={{0,2},{1,3},{2,0},{3,1},{4,6},{5,7},{6,4},{7,5},{8,10},{9,11},{10,... | collective-permute-start | bytes 2359304 | tf_op jit(solution)/shard_map/ppermute | solution.py:733
  853.5 25.0 %collective-permute-start.32 = (bf16[512,2048]{1,0:T(8,128)(2,1)S(1)}, bf16[512,2048]{1,0:T(8,128)(2,1)S(1)}, u32[]{:S(2)}, u32[]{:S(2)}) collective-permute-start(bf16[512,2048]{1,0:T(8,128)(2,1)S(1)} %get-tuple-element.239), channel_id=1, source_target_pairs={{0,1},{1,0},{2,3},{3,2},{4,5},{5,4},{6,7},{7,6},{8,9},{9,8},{10,11... | collective-permute-start | bytes 6291464 | tf_op jit(solution)/shard_map/ppermute | solution.py:733
  854.2 34.5 %collective-permute-start.56 = (bf16[128,2,1536]{0,2,1:T(8,128)(2,1)S(1)}, bf16[128,2,1536]{0,2,1:T(8,128)(2,1)S(1)}, u32[]{:S(2)}, u32[]{:S(2)}) collective-permute-start(bf16[128,2,1536]{0,2,1:T(8,128)(2,1)S(1)} %pad_maximum_fusion.5), channel_id=1, source_target_pairs={{0,4},{1,5},{2,6},{3,7},{4,0},{5,1},{6,2},{7,3},{8,12},{9,13},{10,... | collective-permute-start | bytes 2359304 | tf_op jit(solution)/shard_map/ppermute | solution.py:733
  887.9 47.6 %collective-permute-start.35 = (bf16[512,2048]{1,0:T(8,128)(2,1)}, bf16[512,2048]{1,0:T(8,128)(2,1)}, u32[]{:S(2)}, u32[]{:S(2)}) collective-permute-start(bf16[512,2048]{1,0:T(8,128)(2,1)} %fusion.11), channel_id=1, source_target_pairs={{0,4},{1,5},{2,6},{3,7},{4,0},{5,1},{6,2},{7,3},{8,12},{9,13},{10,... | collective-permute-start | bytes 6291464 | tf_op jit(solution)/shard_map/ppermute | solution.py:733
  894.2 26.5 %collective-permute-start.38 = (bf16[256,1536]{1,0:T(8,128)(2,1)S(1)}, bf16[256,1536]{1,0:T(8,128)(2,1)S(1)}, u32[]{:S(2)}, u32[]{:S(2)}) collective-permute-start(bf16[256,1536]{1,0:T(8,128)(2,1)S(1)} %fusion.27), channel_id=1, source_target_pairs={{0,8},{1,9},{2,10},{3,11},{4,12},{5,13},{6,14},{7,15},{8,16},{9,17... | collective-permute-start | bytes 2359304 | tf_op jit(solution)/shard_map/ppermute | solution.py:733
  895.2 25.5 %collective-permute-start.37 = (bf16[272,1024]{1,0:T(8,128)(2,1)}, bf16[272,1024]{1,0:T(8,128)(2,1)S(1)}, u32[]{:S(2)}, u32[]{:S(2)}) collective-permute-start(bf16[272,1024]{1,0:T(8,128)(2,1)} %get-tuple-element.252), channel_id=1, source_target_pairs={{0,2},{1,3},{2,0},{3,1},{4,6},{5,7},{6,4},{7,5},{8,10},{9,11},{10,... | collective-permute-start | bytes 1671176 | tf_op jit(solution)/shard_map/ppermute | solution.py:733
  938.2 38.4 %collective-permute-start.57 = (bf16[128,1536]{0,1:T(8,128)(2,1)}, bf16[128,1536]{0,1:T(8,128)(2,1)}, u32[]{:S(2)}, u32[]{:S(2)}) collective-permute-start(bf16[128,1536]{0,1:T(8,128)(2,1)} %bitcast.451), channel_id=1, source_target_pairs={{0,1},{1,0},{2,3},{3,2},{4,5},{5,4},{6,7},{7,6},{8,9},{9,8},{10,11... | collective-permute-start | bytes 1179656 | tf_op jit(solution)/shard_map/ppermute | solution.py:733
  942.7 26.3 %collective-permute-start.39 = (bf16[272,1024]{1,0:T(8,128)(2,1)}, bf16[272,1024]{1,0:T(8,128)(2,1)}, u32[]{:S(2)}, u32[]{:S(2)}) collective-permute-start(bf16[272,1024]{1,0:T(8,128)(2,1)} %get-tuple-element.258), channel_id=1, source_target_pairs={{0,2},{1,3},{2,0},{3,1},{4,6},{5,7},{6,4},{7,5},{8,10},{9,11},{10,... | collective-permute-start | bytes 1671176 | tf_op jit(solution)/shard_map/ppermute | solution.py:733
  943.2 25.8 %collective-permute-start.40 = (bf16[272,1024]{1,0:T(8,128)(2,1)}, bf16[272,1024]{1,0:T(8,128)(2,1)}, u32[]{:S(2)}, u32[]{:S(2)}) collective-permute-start(bf16[272,1024]{1,0:T(8,128)(2,1)} %fusion.47), channel_id=1, source_target_pairs={{0,8},{1,9},{2,10},{3,11},{4,12},{5,13},{6,14},{7,15},{8,16},{9,17... | collective-permute-start | bytes 1671176 | tf_op jit(solution)/shard_map/ppermute | solution.py:733
  (93 other events, 1441.1 us)
